TPU v7x, 128 devices: a whole 4x4x4 slice. The times are simulated.
128 devices in a mesh: ctx: 16 (over z, y), tp: 8 (over x, core).
Axes of the slice: x: 4, y: 4, z: 4, core: 2. Of those that a mesh axis runs over, the one named last changes fastest.
Arguments:
- q_in: bfloat16 [8192, 8192], P('ctx', 'tp'), may hold values from -600 to 600
- k_in: bfloat16 [8192, 8192], P('ctx', 'tp'), may hold values from -6 to 6
- v_in: bfloat16 [8192, 8192], P('ctx', 'tp'), may hold values from -6 to 6
- short_weight: float32 [3, 7, 8192], P(None, None, 'tp'), may hold values from -2 to 2
- decay_rate: float32 [64, 16], P('tp'), may hold values from 2.4414063e-05 to 0.0333333333
- residue: float32 [64, 16], P('tp'), may hold values from -2 to 2
- skip: float32 [8192], P('tp'), may hold values from -6 to 6
- gain: float32 [8192], P('tp'), may hold values from 0.25 to 1.75
- d_out: bfloat16 [8192, 8192], P('ctx', 'tp'), may hold values from -12 to 12
Outputs:
- mixed: bfloat16 [8192, 8192], P('ctx', 'tp')
- grad_q: bfloat16 [8192, 8192], P('ctx', 'tp')
- grad_k: bfloat16 [8192, 8192], P('ctx', 'tp')
- grad_v: bfloat16 [8192, 8192], P('ctx', 'tp')
All inputs are finite; a program needn't handle non-finite values.
Results may differ from a plain program's by a relative error of at most 0.0049.
Values may be sent and summed in bfloat16 or wider, within the bound.
A program may use at most 128 MiB of HBM per device.

v0:
```python
import jax
import jax.numpy as jnp
from jax import lax
from jax.sharding import PartitionSpec as P

D = 8192
GROUP_CH = 128
MODES = 16
KER = 7
BLK = 256


PRECISE = lax.Precision.HIGHEST
EPSILON = 1e-05


def from_behind(x, axis, by):
    peers = lax.axis_size(axis)
    pairs = [(i, i + by) for i in range(peers) if 0 <= i + by < peers]
    return lax.ppermute(x, axis, pairs)


def filter_table(decay_rate, residue):
    return residue * jnp.sqrt(-jnp.expm1(-2.0 * decay_rate))


def toeplitz_tile(rate_table, coef_table):
    offset = jnp.arange(BLK)[:, None] - jnp.arange(BLK)[None, :]
    lag_matrix = jnp.maximum(offset, 0).astype(jnp.float32)
    mode_count = rate_table.shape[1]
    summed = coef_table[:, 0, None, None] * jnp.exp(
        -rate_table[:, 0, None, None] * lag_matrix[None]
    )
    for mode_index in range(1, mode_count):
        summed = summed + coef_table[:, mode_index, None, None] * jnp.exp(
            -rate_table[:, mode_index, None, None] * lag_matrix[None]
        )
    return jnp.where(offset[None] >= 0, summed, 0.0)


def block_terms(signal, rate_table, coef_table):
    row_count, groups, group_width = signal.shape
    blocks = row_count // BLK
    pieces = signal.reshape(blocks, BLK, groups, group_width)
    lag_values = jnp.arange(BLK).astype(jnp.float32)
    toeplitz = toeplitz_tile(rate_table, coef_table)
    within = jnp.einsum("gij,bjgc->bigc", toeplitz, pieces, precision=PRECISE)
    tail_decay = jnp.exp(-rate_table[:, :, None] * (BLK - 1 - lag_values))
    block_ends = jnp.einsum("gmj,bjgc->bgmc", tail_decay, pieces, precision=PRECISE)
    return (within, block_ends)


def finish(within, block_ends, rate_table, coef_table, entering):
    blocks, _, groups, group_width = within.shape
    positions = jnp.arange(blocks)
    block_gap = positions[:, None] - 1 - positions[None, :]
    spans = (BLK * jnp.maximum(block_gap, 0)).astype(jnp.float32)
    mixing = jnp.where(
        block_gap[None, None] >= 0, jnp.exp(-rate_table[:, :, None, None] * spans), 0.0
    )
    entry_decay = jnp.exp(-rate_table[None] * (BLK * positions).astype(jnp.float32)[:, None, None])
    starts = (
        jnp.einsum("gmab,bgmc->agmc", mixing, block_ends, precision=PRECISE)
        + entry_decay[..., None] * entering[None]
    )
    lag_values = jnp.arange(BLK).astype(jnp.float32)
    lead_decay = coef_table[:, :, None] * jnp.exp(-rate_table[:, :, None] * (lag_values + 1.0))
    across = jnp.einsum("gmi,bgmc->bigc", lead_decay, starts, precision=PRECISE)
    return (within + across).reshape(blocks * BLK, groups, group_width)


def regrouped(received, rate_table, coef_table, backward):
    row_count, piece_width = received.shape
    sub_width = min(piece_width, GROUP_CH)
    sub_count = piece_width // sub_width
    leading = lax.axis_index("ctx") * piece_width
    member = (leading + jnp.arange(sub_count) * sub_width) // GROUP_CH
    onehot = (member[:, None] == jnp.arange(rate_table.shape[0])[None, :]).astype(jnp.float32)
    own_rates = jnp.dot(onehot, rate_table, precision=PRECISE)
    own_coefs = jnp.dot(onehot, coef_table, precision=PRECISE)
    signal = received.astype(jnp.float32)
    if backward:
        signal = signal[::-1]
    within, block_ends = block_terms(
        signal.reshape(row_count, sub_count, sub_width), own_rates, own_coefs
    )
    empty_state = jnp.zeros((sub_count, MODES, sub_width), jnp.float32)
    result = finish(within, block_ends, own_rates, own_coefs, empty_state).reshape(
        row_count, piece_width
    )
    if backward:
        result = result[::-1]
    return result


def causal_taps(extended, weights, length):
    summed = weights[0] * extended[KER - 1 : KER - 1 + length]
    for tap_index in range(1, KER):
        summed = (
            summed
            + weights[tap_index] * extended[KER - 1 - tap_index : KER - 1 - tap_index + length]
        )
    return summed


def later_taps(extended, weights, length):
    summed = weights[0] * extended[0:length]
    for tap_index in range(1, KER):
        summed = summed + weights[tap_index] * extended[tap_index : tap_index + length]
    return summed


def body(q_in, k_in, v_in, short_weight, decay_rate, residue, skip, gain, d_out):
    length, channels = q_in.shape
    margin = KER - 1
    rim_q, rim_k, rim_v = from_behind(
        (q_in[length - margin :], k_in[length - margin :], v_in[length - margin :]), "ctx", 1
    )
    q_short = causal_taps(
        jnp.concatenate([rim_q, q_in], 0).astype(jnp.float32), short_weight[0], length
    )
    k_short = causal_taps(
        jnp.concatenate([rim_k, k_in], 0).astype(jnp.float32), short_weight[1], length
    )
    v_short = causal_taps(
        jnp.concatenate([rim_v, v_in], 0).astype(jnp.float32), short_weight[2], length
    )
    product = (k_short * v_short).astype(jnp.bfloat16)
    product_wide = product.astype(jnp.float32)
    coef_table = filter_table(decay_rate, residue)
    received = lax.all_to_all(product, "ctx", split_axis=1, concat_axis=0, tiled=True)
    carried_parts = regrouped(received, decay_rate, coef_table, False)
    carried = lax.all_to_all(carried_parts, "ctx", split_axis=0, concat_axis=1, tiled=True)
    filtered = carried + skip * product_wide
    gated = q_short * filtered
    d_scaled = d_out.astype(jnp.float32) * gain
    squares, aligned = lax.psum(
        (jnp.sum(gated * gated, axis=1), jnp.sum(d_scaled * gated, axis=1)), "tp"
    )
    scale = lax.rsqrt(squares / D + EPSILON)
    cross_mean = aligned / D
    mixed = (gated * scale[:, None] * gain).astype(jnp.bfloat16)
    d_gated = scale[:, None] * d_scaled - (scale**3 * cross_mean)[:, None] * gated
    dq_short = d_gated * filtered
    d_filtered = (d_gated * q_short).astype(jnp.bfloat16)
    d_filtered_wide = d_filtered.astype(jnp.float32)
    received_back = lax.all_to_all(d_filtered, "ctx", split_axis=1, concat_axis=0, tiled=True)
    back_parts = regrouped(received_back, decay_rate, coef_table, True)
    carried_back = lax.all_to_all(back_parts, "ctx", split_axis=0, concat_axis=1, tiled=True)
    d_product = carried_back + skip * d_filtered_wide
    dk_short = d_product * v_short
    dv_short = d_product * k_short
    next_q, next_k, next_v = from_behind(
        (dq_short[:margin], dk_short[:margin], dv_short[:margin]), "ctx", -1
    )
    grad_q = later_taps(jnp.concatenate([dq_short, next_q], 0), short_weight[0], length).astype(
        jnp.bfloat16
    )
    grad_k = later_taps(jnp.concatenate([dk_short, next_k], 0), short_weight[1], length).astype(
        jnp.bfloat16
    )
    grad_v = later_taps(jnp.concatenate([dv_short, next_v], 0), short_weight[2], length).astype(
        jnp.bfloat16
    )
    return (mixed, grad_q, grad_k, grad_v)


def solution(mesh):
    in_specs = (
        P("ctx", "tp"),
        P("ctx", "tp"),
        P("ctx", "tp"),
        P(None, None, "tp"),
        P("tp", None),
        P("tp", None),
        P("tp"),
        P("tp"),
        P("ctx", "tp"),
    )
    out_specs = (P("ctx", "tp"), P("ctx", "tp"), P("ctx", "tp"), P("ctx", "tp"))
    return jax.shard_map(body, mesh=mesh, in_specs=in_specs, out_specs=out_specs, check_vma=False)
```

profile of v0, /device:TPU:22, one launch (start us, length us, event | category | flops | bytes accessed | tf_op | source)
XLA Modules:
  0.0 336.2 jit_solution(18198584253342465027)
XLA Ops:
  6.5 3.5 %collective-permute-start.2 = (bf16[6,1024]{0,1:T(8,128)(2,1)}, bf16[6,1024]{0,1:T(8,128)(2,1)}, u32[]{:S(2)}, u32[]{:S(2)}) collective-permute-start(bf16[6,1024]{0,1:T(8,128)(2,1)} %copy.46), channel_id=1, source_target_pairs={{0,8},{8,16},{16,24},{24,32},{32,40},{40,48},{48,56},{56,64},{64,7... | collective-permute-start | bytes 36872 | tf_op jit(solution)/shard_map/ppermute | solution.py:20
  29.0 10.3 %multiply_convert_fusion.2 = (bf16[512,1024]{0,1:T(8,128)(2,1)}, f32[512,1024]{0,1:T(8,128)}, f32[512,1024]{0,1:T(8,128)}) fusion(f32[518,1024]{0,1:T(8,128)S(1)} %maximum_convert_fusion.2, f32[1024]{0:T(1024)S(1)} %bitcast.223, f32[1024]{0:T(1024)S(1)} %bitcast.221, f32[1024]{0:T(1024)S(1)} %bitcast.197, f32[1024]{0:T(1024)S(1)} %bitcast.199, ...), kind=kLoop, calls=%fused_computation.141 | loop fusion | flops 14680064 | bytes 34660352 | tf_op jit(solution)/shard_map/convert_element_type | solution.py:128
  39.4 8.1 %all-to-all-start = ((bf16[512,16,64]{0,2,1:T(8,128)(2,1)}), bf16[512,16,64]{0,2,1:T(8,128)(2,1)S(1)}, u32[]{:S(2)}, u32[]{:S(2)}) async-start(bf16[512,16,64]{0,2,1:T(8,128)(2,1)} %bitcast.21), calls=%async_computation | async-start | bytes 2097152 | tf_op jit(solution)/shard_map/all_to_all | solution.py:131
  48.5 12.9 %all-to-all-done = bf16[512,16,64]{0,2,1:T(8,128)(2,1)S(1)} async-done(((bf16[512,16,64]{0,2,1:T(8,128)(2,1)}), bf16[512,16,64]{0,2,1:T(8,128)(2,1)S(1)}, u32[]{:S(2)}, u32[]{:S(2)}) %all-to-all-start) | async-done | bytes 1048608 | tf_op jit(solution)/shard_map/all_to_all | solution.py:131
  65.7 12.4 %fusion.85 = f32[32,64,256]{2,1,0:T(8,128)S(1)} fusion(bf16[32,256,64]{1,0,2:T(8,128)(2,1)S(1)} %reshape.863, f32[]{:T(128)} %bitcast.60, f32[]{:T(128)} %bitcast.59, f32[]{:T(128)} %bitcast.58, f32[]{:T(128)} %bitcast.57, f32[]{:T(128)} %bitcast.56, f32[]{:T(128)} %bitcast.55, f32[]{:T(128)} %bitcast.54, f32[]{:T(128)} %bitcast.53, f32[]{:T(128)} %bitcast.52, ...), kind=kOutput, calls=%fused_computation.157 | convolution fusion | flops 1614020608 | bytes 3145856 | tf_op jit(solution)/shard_map/gij,bjgc->bigc/dot_general | solution.py:47
  82.9 4.1 %copy.53 = f32[16,512,64]{1,2,0:T(8,128)} copy(f32[16,512,64]{1,0,2:T(8,128)} %all_to_all.53) | data formatting | bytes 4194304 | tf_op jit(solution)/shard_map/all_to_all | solution.py:133
  87.0 7.4 %all-to-all-start.1 = ((f32[16,512,64]{1,2,0:T(8,128)}), f32[16,512,64]{1,2,0:T(8,128)}, u32[]{:S(2)}, u32[]{:S(2)}) async-start(f32[16,512,64]{1,2,0:T(8,128)} %copy.53), calls=%async_computation.1 | async-start | bytes 4194304 | tf_op jit(solution)/shard_map/all_to_all | solution.py:133
  100.8 23.1 %collective-permute-done = bf16[6,1024]{0,1:T(8,128)(2,1)S(1)} collective-permute-done((bf16[6,1024]{0,1:T(8,128)(2,1)S(1)}, bf16[6,1024]{0,1:T(8,128)(2,1)S(1)}, u32[]{:S(2)}, u32[]{:S(2)}) %collective-permute-start) | collective-permute-done | bytes 12320 | tf_op jit(solution)/shard_map/ppermute | solution.py:20
  125.7 7.6 %multiply_reduce_fusion = (f32[512]{0:T(512)S(1)}, f32[512]{0:T(512)S(1)}, f32[512,1024]{0,1:T(8,128)}, f32[512,1024]{0,1:T(8,128)}) fusion(bf16[512,1024]{0,1:T(8,128)(2,1)} %copy.54, f32[1024]{0:T(1024)S(1)} %copy-done.8, bf16[512,1024]{0,1:T(8,128)(2,1)} %get-tuple-element.18, f32[1024]{0:T(1024)S(1)} %copy-done.6, f32[16,512,64]{1,2,0:T(8,128)} %all-to-all-done.1, ...), kind=kLoop, calls=%fused_computation.136 | loop fusion | flops 12057600 | bytes 23109632 | tf_op jit(solution)/shard_map/reduce_sum | solution.py:138
  133.3 10.6 %all-reduce = (f32[512]{0:T(512)S(1)}, f32[512]{0:T(512)S(1)}) all-reduce(f32[512]{0:T(512)S(1)} %get-tuple-element.13, f32[512]{0:T(512)S(1)} %get-tuple-element.12), channel_id=1, replica_groups=mesh['ctx'=16,'tp'=8] {'tp'}, use_global_device_ids=true, to_apply=%region_1.2 | all-reduce | flops 1024 | bytes 8192 | tf_op jit(solution)/shard_map/psum | solution.py:137
  143.9 5.1 %multiply_convert_fusion = (bf16[512,1024]{0,1:T(8,128)(2,1)S(1)}, f32[512,1024]{0,1:T(8,128)}, bf16[512,1024]{0,1:T(8,128)(2,1)}) fusion(f32[512,1024]{0,1:T(8,128)} %get-tuple-element.17, f32[512,1024]{0,1:T(8,128)} %get-tuple-element.16, bf16[512,1024]{0,1:T(8,128)(2,1)} %copy.54, f32[512]{0:T(512)S(1)} %get-tuple-element.47, f32[1024]{0:T(1024)S(1)} %copy-done.8, ...), kind=kLoop, calls=%fused_computation.134 | loop fusion | flops 7340032 | bytes 12595200 | tf_op jit(solution)/shard_map/convert_element_type | solution.py:145
  149.1 23.3 %all_to_all.67 = bf16[512,16,64]{0,2,1:T(8,128)(2,1)S(1)} all-to-all(bf16[512,16,64]{0,2,1:T(8,128)(2,1)S(1)} %bitcast.189), channel_id=1, replica_groups=mesh['ctx'=16,'tp'=8] {'ctx'}, dimensions={1} | all-to-all | bytes 2097152 | tf_op jit(solution)/shard_map/all_to_all | solution.py:147
  174.2 26.8 %rev.6 = f32[8192,64]{0,1:T(8,128)S(1)} reverse(f32[8192,64]{0,1:T(8,128)} %bitcast.190), dimensions={0} | reverse | bytes 4194304 | tf_op jit(solution)/shard_map/rev | solution.py:83
  201.6 4.2 %convolution_bitcast_fusion = f32[32,16,64]{0,1,2:T(8,128)S(1)} fusion(f32[32,256,64]{1,0,2:T(8,128)S(1)} %bitcast.191, f32[256]{0:T(256)S(1)} %convert_subtract_fusion, f32[16]{0:T(128)S(1)} %get-tuple-element.81), kind=kOutput, calls=%fused_computation.149 | convolution fusion | flops 100667392 | bytes 2229312 | tf_op jit(solution)/shard_map/gmj,bjgc->bgmc/dot_general | solution.py:49
  208.8 12.3 %fusion.150 = f32[8,8,32,256]{3,1,0,2:T(8,128)S(1)} fusion(f32[32,64,256]{2,1,0:T(8,128)S(1)} %fusion.91, f32[]{:T(128)} %bitcast.60, f32[]{:T(128)} %bitcast.59, f32[]{:T(128)} %bitcast.58, f32[]{:T(128)} %bitcast.57, f32[]{:T(128)} %bitcast.56, f32[]{:T(128)} %bitcast.55, f32[]{:T(128)} %bitcast.54, f32[]{:T(128)} %bitcast.53, f32[]{:T(128)} %bitcast.52, ...), kind=kOutput, calls=%fused_computation.233 | convolution fusion | flops 1614544896 | bytes 6291584 | tf_op jit(solution)/shard_map/gij,bjgc->bigc/dot_general | solution.py:47
  221.3 22.4 %rev.7 = f32[8192,64]{0,1:T(8,128)} reverse(f32[8192,64]{0,1:T(8,128)S(1)} %bitcast.192), dimensions={0} | reverse | bytes 4194304 | tf_op jit(solution)/shard_map/rev | solution.py:92
  247.0 7.1 %all-to-all-start.3 = ((f32[16,512,64]{1,2,0:T(8,128)}), f32[16,512,64]{1,2,0:T(8,128)}, u32[]{:S(2)}, u32[]{:S(2)}) async-start(f32[16,512,64]{1,2,0:T(8,128)} %bitcast.186), calls=%async_computation.3 | async-start | bytes 4194304 | tf_op jit(solution)/shard_map/all_to_all | solution.py:149
  259.9 23.1 %all-to-all-done.3 = f32[16,512,64]{1,2,0:T(8,128)} async-done(((f32[16,512,64]{1,2,0:T(8,128)}), f32[16,512,64]{1,2,0:T(8,128)}, u32[]{:S(2)}, u32[]{:S(2)}) %all-to-all-start.3) | async-done | bytes 2097184 | tf_op jit(solution)/shard_map/all_to_all | solution.py:149
  283.0 4.6 %fusion.79 = (f32[512,1024]{0,1:T(8,128)}, f32[512,1024]{0,1:T(8,128)S(1)}) fusion(f32[512,1024]{0,1:T(8,128)} %get-tuple-element.20, bf16[512,1024]{0,1:T(8,128)(2,1)S(1)} %get-tuple-element.21, f32[16,512,64]{1,2,0:T(8,128)} %all-to-all-done.3, f32[1024]{0:T(1024)S(1)} %copy-done.6, f32[512,1024]{0,1:T(8,128)} %get-tuple-element.19), kind=kLoop, calls=%fused_computation.144 | loop fusion | flops 2621440 | bytes 11538432 | tf_op jit(solution)/shard_map/mul | solution.py:152
  289.8 3.7 %collective-permute-start.4 = (f32[6,1024]{0,1:T(8,128)}, f32[6,1024]{0,1:T(8,128)}, u32[]{:S(2)}, u32[]{:S(2)}) collective-permute-start(f32[6,1024]{0,1:T(8,128)} %slice.525), channel_id=1, source_target_pairs={{8,0},{16,8},{24,16},{32,24},{40,32},{48,40},{56,48},{64,56},{72,6... | collective-permute-start | bytes 73736 | tf_op jit(solution)/shard_map/ppermute | solution.py:20
  293.6 8.4 %fusion.38 = bf16[512,1024]{0,1:T(8,128)(2,1)S(1)} fusion(f32[512,1024]{0,1:T(8,128)S(1)} %copy-done, f32[6,1024]{0,1:T(8,128)} %collective-permute-done.3, f32[1024]{0:T(1024)S(1)} %bitcast.228, f32[1024]{0:T(1024)S(1)} %bitcast.230, f32[1024]{0:T(1024)S(1)} %bitcast.232, f32[1024]{0:T(1024)S(1)} %bitcast.234, f32[1024]{0:T(1024)S(1)} %bitcast.236, ...), kind=kLoop, calls=%fused_computation.68 | loop fusion | flops 10485760 | bytes 3198976 | tf_op jit(solution)/shard_map/convert_element_type | solution.py:156
  305.2 7.3 %collective-permute-start.5 = (f32[6,1024]{0,1:T(8,128)}, f32[6,1024]{0,1:T(8,128)}, u32[]{:S(2)}, u32[]{:S(2)}) collective-permute-start(f32[6,1024]{0,1:T(8,128)} %slice.536), channel_id=1, source_target_pairs={{8,0},{16,8},{24,16},{32,24},{40,32},{48,40},{56,48},{64,56},{72,6... | collective-permute-start | bytes 73736 | tf_op jit(solution)/shard_map/ppermute | solution.py:20
  312.5 12.8 %fusion.21 = bf16[512,1024]{0,1:T(8,128)(2,1)S(1)} fusion(f32[512,1024]{0,1:T(8,128)} %copy-done.2, f32[6,1024]{0,1:T(8,128)} %collective-permute-done.4, f32[1024]{0:T(1024)S(1)} %bitcast.208, f32[1024]{0:T(1024)S(1)} %bitcast.210, f32[1024]{0:T(1024)S(1)} %bitcast.212, f32[1024]{0:T(1024)S(1)} %bitcast.214, f32[1024]{0:T(1024)S(1)} %bitcast.216, ...), kind=kLoop, calls=%fused_computation.51 | loop fusion | flops 10485760 | bytes 3198976 | tf_op jit(solution)/shard_map/convert_element_type | solution.py:159
  326.6 8.2 %fusion.4 = bf16[512,1024]{0,1:T(8,128)(2,1)S(1)} fusion(f32[512,1024]{0,1:T(8,128)S(1)} %copy-done.1, f32[6,1024]{0,1:T(8,128)} %collective-permute-done.5, f32[1024]{0:T(1024)S(1)} %bitcast.224, f32[1024]{0:T(1024)S(1)} %bitcast.222, f32[1024]{0:T(1024)S(1)} %bitcast.198, f32[1024]{0:T(1024)S(1)} %bitcast.200, f32[1024]{0:T(1024)S(1)} %bitcast.202, ...), kind=kLoop, calls=%fused_computation.34 | loop fusion | flops 10485760 | bytes 3198976 | tf_op jit(solution)/shard_map/convert_element_type | solution.py:162
  (77 shorter events, 55.6 us)
Async XLA Ops:
  0.6 14.7 %copy-start.3 = (bf16[512,1024]{1,0:T(8,128)(2,1)S(1)}, bf16[512,1024]{1,0:T(8,128)(2,1)}, u32[]{:S(2)}) copy-start(bf16[512,1024]{1,0:T(8,128)(2,1)} %param.11) | copy-start | bytes 3145732
  1.7 25.8 %collective-permute-start.1 = (bf16[6,1024]{0,1:T(8,128)(2,1)S(1)}, bf16[6,1024]{0,1:T(8,128)(2,1)}, u32[]{:S(2)}, u32[]{:S(2)}) collective-permute-start(bf16[6,1024]{0,1:T(8,128)(2,1)S(1)} %copy.44), channel_id=1, source_target_pairs={{0,8},{8,16},{16,24},{24,32},{32,40},{40,48},{48,56},{56,64},{64,7... | collective-permute-start | bytes 36872 | tf_op jit(solution)/shard_map/ppermute | solution.py:20
  6.5 19.5 %collective-permute-start.2 = (bf16[6,1024]{0,1:T(8,128)(2,1)}, bf16[6,1024]{0,1:T(8,128)(2,1)}, u32[]{:S(2)}, u32[]{:S(2)}) collective-permute-start(bf16[6,1024]{0,1:T(8,128)(2,1)} %copy.46), channel_id=1, source_target_pairs={{0,8},{8,16},{16,24},{24,32},{32,40},{40,48},{48,56},{56,64},{64,7... | collective-permute-start | bytes 36872 | tf_op jit(solution)/shard_map/ppermute | solution.py:20
  39.4 8.1 %copy-start.7 = (f32[8,16]{1,0:T(8,128)S(1)}, f32[8,16]{1,0:T(8,128)}, u32[]{:S(2)}) copy-start(f32[8,16]{1,0:T(8,128)} %param.13) | copy-start | bytes 1540
  39.4 8.1 %copy-start.9 = (f32[8,16]{1,0:T(8,128)S(1)}, f32[8,16]{1,0:T(8,128)}, u32[]{:S(2)}) copy-start(f32[8,16]{1,0:T(8,128)} %param.14) | copy-start | bytes 1540
  39.4 22.1 %all-to-all-start = ((bf16[512,16,64]{0,2,1:T(8,128)(2,1)}), bf16[512,16,64]{0,2,1:T(8,128)(2,1)S(1)}, u32[]{:S(2)}, u32[]{:S(2)}) async-start(bf16[512,16,64]{0,2,1:T(8,128)(2,1)} %bitcast.21), calls=%async_computation | async-start | bytes 2097152 | tf_op jit(solution)/shard_map/all_to_all | solution.py:131
  87.0 7.4 %copy-start.4 = (bf16[512,1024]{1,0:T(8,128)(2,1)S(1)}, bf16[512,1024]{1,0:T(8,128)(2,1)}, u32[]{:S(2)}) copy-start(bf16[512,1024]{1,0:T(8,128)(2,1)} %param.9) | copy-start | bytes 3145732
  87.0 38.7 %all-to-all-start.1 = ((f32[16,512,64]{1,2,0:T(8,128)}), f32[16,512,64]{1,2,0:T(8,128)}, u32[]{:S(2)}, u32[]{:S(2)}) async-start(f32[16,512,64]{1,2,0:T(8,128)} %copy.53), calls=%async_computation.1 | async-start | bytes 4194304 | tf_op jit(solution)/shard_map/all_to_all | solution.py:133
  94.5 5.0 %copy-start.5 = (bf16[512,1024]{1,0:T(8,128)(2,1)S(1)}, bf16[512,1024]{1,0:T(8,128)(2,1)}, u32[]{:S(2)}) copy-start(bf16[512,1024]{1,0:T(8,128)(2,1)} %param.17) | copy-start | bytes 3145732
  94.7 29.2 %collective-permute-start = (bf16[6,1024]{0,1:T(8,128)(2,1)S(1)}, bf16[6,1024]{0,1:T(8,128)(2,1)S(1)}, u32[]{:S(2)}, u32[]{:S(2)}) collective-permute-start(bf16[6,1024]{0,1:T(8,128)(2,1)S(1)} %copy.42), channel_id=1, source_target_pairs={{0,8},{8,16},{16,24},{24,32},{32,40},{40,48},{48,56},{56,64},{64,7... | collective-permute-start | bytes 36872 | tf_op jit(solution)/shard_map/ppermute | solution.py:20
  100.8 24.9 %copy-start.6 = (f32[1024]{0:T(1024)S(1)}, f32[1024]{0:T(1024)}, u32[]{:S(2)}) copy-start(f32[1024]{0:T(1024)} %param.15) | copy-start | bytes 12292
  100.8 24.9 %copy-start.8 = (f32[1024]{0:T(1024)S(1)}, f32[1024]{0:T(1024)}, u32[]{:S(2)}) copy-start(f32[1024]{0:T(1024)} %param.16) | copy-start | bytes 12292
  247.0 36.0 %all-to-all-start.3 = ((f32[16,512,64]{1,2,0:T(8,128)}), f32[16,512,64]{1,2,0:T(8,128)}, u32[]{:S(2)}, u32[]{:S(2)}) async-start(f32[16,512,64]{1,2,0:T(8,128)} %bitcast.186), calls=%async_computation.3 | async-start | bytes 4194304 | tf_op jit(solution)/shard_map/all_to_all | solution.py:149
  254.1 2.4 copy-start
  257.4 36.2 %collective-permute-start.3 = (f32[6,1024]{0,1:T(8,128)}, f32[6,1024]{0,1:T(8,128)}, u32[]{:S(2)}, u32[]{:S(2)}) collective-permute-start(f32[6,1024]{0,1:T(8,128)} %slice.514), channel_id=1, source_target_pairs={{8,0},{16,8},{24,16},{32,24},{40,32},{48,40},{56,48},{64,56},{72,6... | collective-permute-start | bytes 73736 | tf_op jit(solution)/shard_map/ppermute | solution.py:20
  287.6 1.3 copy-start.2
  289.8 22.7 %collective-permute-start.4 = (f32[6,1024]{0,1:T(8,128)}, f32[6,1024]{0,1:T(8,128)}, u32[]{:S(2)}, u32[]{:S(2)}) collective-permute-start(f32[6,1024]{0,1:T(8,128)} %slice.525), channel_id=1, source_target_pairs={{8,0},{16,8},{24,16},{32,24},{40,32},{48,40},{56,48},{64,56},{72,6... | collective-permute-start | bytes 73736 | tf_op jit(solution)/shard_map/ppermute | solution.py:20
  305.2 21.4 %copy-start.1 = (f32[512,1024]{0,1:T(8,128)S(1)}, f32[512,1024]{0,1:T(8,128)}, u32[]{:S(2)}) copy-start(f32[512,1024]{0,1:T(8,128)} %get-tuple-element.23) | copy-start | bytes 6291460
  305.2 21.4 %collective-permute-start.5 = (f32[6,1024]{0,1:T(8,128)}, f32[6,1024]{0,1:T(8,128)}, u32[]{:S(2)}, u32[]{:S(2)}) collective-permute-start(f32[6,1024]{0,1:T(8,128)} %slice.536), channel_id=1, source_target_pairs={{8,0},{16,8},{24,16},{32,24},{40,32},{48,40},{56,48},{64,56},{72,6... | collective-permute-start | bytes 73736 | tf_op jit(solution)/shard_map/ppermute | solution.py:20
where the time goes:
time: 340 us; the launch traced here: 336 us
  local copies, waits for them, and re-layouts  85.4 us (25%)
  other arithmetic  62.5 us (18%)
  waiting for transfers between devices  59.2 us (17%)
  starting transfers between devices  46.2 us (14%)
  matrix products  38 us (11%)
  blocking collectives  33.8 us (10%)
  between operations  11.1 us (3%)
    rev x1, local copies, waits for them, and re-layouts, regrouped(): signal = signal[::-1]  26.8 us
    dot_general x2, matrix products, block_terms(): within = jnp.einsum('gij,bjgc->bigc', toeplitz, pieces, precision=PRECISE)  24.7 us
    ppermute x6, starting transfers between devices, from_behind(): return lax.ppermute(x, axis, pairs)  23.6 us
    all_to_all x1, blocking collectives, body(): lax.all_to_all(d_filtered, 'ctx', split_axis=1, concat_axis=0, tiled=True)  23.3 us
    ppermute x6, waiting for transfers between devices, from_behind(): return lax.ppermute(x, axis, pairs)  23.1 us
    all_to_all x1, waiting for transfers between devices, body(): lax.all_to_all(back_parts, 'ctx', split_axis=0, concat_axis=1, tiled=True)  23.1 us
    rev x1, local copies, waits for them, and re-layouts, regrouped(): result = result[::-1]  22.4 us
    unnamed x30, local copies, waits for them, and re-layouts  13.2 us
  transfers between devices with their start and end apart: 9, of which 3 were waited for; matrix products, arithmetic and copies ran while one was open for 15% of the time, Pallas kernels for 0%

commit v1 on v0

v1 whole, which is shorter than its diff:
```python
import functools

import jax
import jax.numpy as jnp
from jax import lax
from jax.experimental import pallas as pl
from jax.experimental.pallas import tpu as pltpu
from jax.sharding import PartitionSpec as P

KER = 7
MODES = 16
GROUP_CH = 128
EPSILON = 1e-05
NZ = 4
NY = 4
ROWS = 64
MESH = pl.DeviceIdType.MESH
F32 = jnp.float32
BF16 = jnp.bfloat16


def split(x):
    hi = x.astype(BF16)
    lo = (x - hi.astype(F32)).astype(BF16)
    return hi, lo


def mm(a, b):
    return jnp.dot(a, b, preferred_element_type=F32)


def kernel(
    ntp,
    q_hbm, k_hbm, v_hbm, d_hbm, w_hbm, rate_hbm, res_hbm, skip_hbm, gain_hbm,
    mixed_hbm, gq_hbm, gk_hbm, gv_hbm,
    xin, win, ratein, resin, skipin, gainin,
    halo, xs, qs, ks, vs, pb, fw, grads, outs,
    wf, wb, leadf, leadb, tailf, tailb, wts,
    acc, scales, xpart, sy, sz, cs,
    in_sem, par_sem, out_sem,
    hsend, hrecv, ysend, yrecv, zsend, zrecv, csend, crecv, gsend, grecv,
):
    groups = xin.shape[1]
    length = xin.shape[2]
    nctx = NZ * NY
    half = length // 2
    me = lax.axis_index("ctx")
    tp = lax.axis_index("tp")
    z = lax.div(me, NY)
    y = lax.rem(me, NY)
    behind = lax.rem(me + nctx - 1, nctx)
    ahead = lax.rem(me + 1, nctx)

    bar = pltpu.get_barrier_semaphore()

    def greet(c, t):
        pl.semaphore_signal(bar, inc=1, device_id=(c, t), device_id_type=MESH)

    def ypeer(step):
        return z * NY + lax.rem(y + step, NY)

    def zpeer(step):
        return lax.rem(z + step, NZ) * NY + y

    for step in range(1, NY):
        greet(ypeer(step), tp)
    for step in range(1, NZ):
        greet(zpeer(step), tp)
    greet(behind, tp)
    greet(ahead, tp)
    for step in range(1, ntp):
        greet(me, lax.rem(tp + step, ntp))

    params = [
        pltpu.make_async_copy(src, dst, par_sem.at[i])
        for i, (src, dst) in enumerate(
            ((rate_hbm, ratein), (res_hbm, resin), (w_hbm, win), (skip_hbm, skipin), (gain_hbm, gainin))
        )
    ]
    for copy in params:
        copy.start()

    def cols(g):
        return pl.ds(pl.multiple_of(g * GROUP_CH, GROUP_CH), GROUP_CH)

    def load(a, g):
        src = (q_hbm, k_hbm, v_hbm, d_hbm)[a]
        return pltpu.make_async_copy(src.at[:, cols(g)], xin.at[a, g], in_sem.at[a, g])

    for a in range(4):
        @pl.loop(0, groups)
        def _(g):
            load(a, g).start()

    for copy in params:
        copy.wait()

    states = groups * MODES
    rate = ratein[...]
    r2 = rate * rate
    sinhc = 1.0 + r2 * (1 / 6) * (1.0 + r2 * (1 / 20) * (1.0 + r2 * (1 / 42) * (1.0 + r2 * (1 / 72) * (1.0 + r2 * (1 / 110)))))
    coef = resin[...] * jnp.sqrt(2.0 * rate * jnp.exp(-rate) * sinhc)
    row_i = lax.broadcasted_iota(jnp.int32, (MODES, MODES), 0)
    col_i = lax.broadcasted_iota(jnp.int32, (MODES, MODES), 1)

    def column(x):
        parts = [
            jnp.sum(jnp.where(row_i == col_i, jnp.broadcast_to(x[g : g + 1, :], (MODES, MODES)), 0.0), axis=1, keepdims=True)
            for g in range(groups)
        ]
        return jnp.concatenate(parts, axis=0)

    rate_wide = jnp.broadcast_to(column(rate), (states, GROUP_CH))
    coef_wide = jnp.broadcast_to(column(coef), (states, GROUP_CH))
    rate_row = rate_wide.T[0:1, :]
    coef_row = coef_wide.T[0:1, :]

    lag = lax.broadcasted_iota(jnp.int32, (states, GROUP_CH), 1).astype(F32)
    for b in range(length // GROUP_CH):
        at = lag + float(b * GROUP_CH)
        fh, fl = split(jnp.exp(-rate_wide * (float(length - 1) - at)))
        bh, bl = split(jnp.exp(-rate_wide * at))
        c = slice(b * GROUP_CH, (b + 1) * GROUP_CH)
        for g in range(groups):
            m = slice(g * MODES, (g + 1) * MODES)
            tailf[g, 0:MODES, c] = fh[m]
            tailf[g, MODES : 2 * MODES, c] = fl[m]
            tailb[g, 0:MODES, c] = bh[m]
            tailb[g, MODES : 2 * MODES, c] = bl[m]

    t_idx = lax.broadcasted_iota(jnp.int32, (GROUP_CH, states), 0).astype(F32)
    for b in range(length // GROUP_CH):
        at = t_idx + float(b * GROUP_CH)
        r = slice(b * GROUP_CH, (b + 1) * GROUP_CH)
        for lead, expo in ((leadf, at + 1.0), (leadb, float(length) - at)):
            hi, lo = split(coef_row * jnp.exp(-rate_row * expo))
            lead[r, 0:states] = hi
            lead[r, states : 2 * states] = hi
            lead[r, 2 * states : 3 * states] = lo

    for i in range(4):
        fi = jnp.float32(i)
        yf = y.astype(F32)
        zf = z.astype(F32)
        span = rate_wide * float(length)

        def weight(count, live):
            return jnp.where(live, jnp.exp(-span * jnp.maximum(count, 0.0)), 0.0)

        wts[0, i] = weight(yf - 1.0 - fi, i < y)
        wts[1, i] = jnp.exp(-span * float(NY - 1 - i))
        wts[2, i] = weight(NY * (zf - 1.0 - fi) + yf, i < z)
        wts[3, i] = weight(fi - yf - 1.0, i > y)
        wts[4, i] = jnp.exp(-span * float(i))
        wts[5, i] = weight(NY * (fi - zf - 1.0) + (NY - 1.0 - yf), i > z)

    pl.semaphore_wait(bar, 2 + NY - 1 + NZ - 1 + ntp - 1)

    def halo_copy(a):
        src = (q_hbm, k_hbm, v_hbm)[a]
        return pltpu.make_async_remote_copy(
            src_ref=src.at[pl.ds(length - 8, 8), :],
            dst_ref=halo.at[a],
            send_sem=hsend.at[a],
            recv_sem=hrecv.at[a],
            device_id=(ahead, tp),
            device_id_type=MESH,
        )

    for a in (1, 2, 0):
        halo_copy(a).start()

    i_idx = lax.broadcasted_iota(jnp.int32, (half, states), 0)
    lane_group = lax.broadcasted_iota(jnp.int32, (half, states), 1) // MODES
    grow_b = coef_row * jnp.exp(rate_row * i_idx.astype(F32))
    grow_f = coef_row * jnp.exp(rate_row * (float(half - 1) - i_idx.astype(F32)))
    ti = lax.broadcasted_iota(jnp.int32, (half, half), 0)
    tj = lax.broadcasted_iota(jnp.int32, (half, half), 1)
    acc[0, 0:half, :] = grow_f
    acc[1, 0:half, :] = grow_b

    @pl.loop(0, groups)
    def _(g):
        for a, (table, tail) in enumerate(((wf, tailf), (wb, tailb))):
            grow = acc[a, 0:half, :]
            pick = jnp.where(
                lax.broadcasted_iota(jnp.int32, (states, MODES), 0) == g * MODES + lax.broadcasted_iota(jnp.int32, (states, MODES), 1),
                1.0, 0.0,
            ).astype(BF16)
            hi, lo = split(grow)
            hi = mm(hi, pick).astype(BF16)
            lo = mm(lo, pick).astype(BF16)
            for b in range(2):
                c = slice(b * half, (b + 1) * half)
                th = tail[g, 0:MODES, c]
                tl = tail[g, MODES : 2 * MODES, c]
                w = mm(hi, th) + mm(hi, tl) + mm(lo, th)
                if a == 0 and b == 1:
                    w = jnp.where(ti >= tj, w, 0.0)
                if a == 1 and b == 0:
                    w = jnp.where(tj >= ti, w, 0.0)
                table[g, :, c] = w.astype(BF16)

    inner = (me > 0).astype(F32)
    final = (me < nctx - 1).astype(F32)

    def taps(a, g):
        return [win[a, j : j + 1, cols(g)] for j in range(KER)]

    def causal(slot, w, lo, rows):
        total = w[0] * xs[slot, pl.ds(8 + lo, rows), :]
        for j in range(1, KER):
            total = total + w[j] * xs[slot, pl.ds(8 + lo - j, rows), :]
        return total

    def later(a, g, w, lo, rows):
        total = w[0] * grads[a, g, pl.ds(lo, rows), :]
        for j in range(1, KER):
            total = total + w[j] * grads[a, g, pl.ds(lo + j, rows), :]
        return total

    @pl.loop(0, groups)
    def _(g):
        load(0, g).wait()
        for lo in range(0, length, ROWS):
            xs[0, 8 + lo : 8 + lo + ROWS, :] = xin[0, g, lo : lo + ROWS, :].astype(F32)
        w = taps(0, g)
        qs[g, 8:ROWS, :] = causal(0, w, 8, ROWS - 8)
        for lo in range(ROWS, length, ROWS):
            qs[g, lo : lo + ROWS, :] = causal(0, w, lo, ROWS)

    for a in (1, 2, 0):
        halo_copy(a).wait_recv()

    def state_copy(buf, send, recv, mine, d, g, step, peer):
        return pltpu.make_async_remote_copy(
            src_ref=buf.at[d, mine, g],
            dst_ref=buf.at[d, mine, g],
            send_sem=send.at[d, step, g],
            recv_sem=recv.at[d, mine, g],
            device_id=(peer, tp),
            device_id_type=MESH,
        )

    def y_start(d, g):
        for step in (1, 3, 2):
            state_copy(sy, ysend, yrecv, y, d, g, step, ypeer(step)).start()

    def z_start(d, g):
        for step in (1, 3, 2):
            state_copy(sz, zsend, zrecv, z, d, g, step, zpeer(step)).start()

    def arrived(buf, recv, d, g, slot):
        pltpu.make_async_copy(buf.at[d, slot, g], buf.at[d, slot, g], recv.at[d, slot, g]).wait()

    def y_total(d, g):
        m = pl.ds(pl.multiple_of(g * MODES, MODES), MODES)
        for step in (1, 3, 2):
            arrived(sy, yrecv, d, g, lax.rem(y + step, NY))
        part = jnp.zeros((MODES, GROUP_CH), F32)
        total = jnp.zeros((MODES, GROUP_CH), F32)
        for i in range(NY):
            s = sy[d, i, g]
            part = part + wts[3 * d, i, m, :] * s
            total = total + wts[3 * d + 1, i, m, :] * s
        xpart[g] = part
        sz[d, z, g] = total
        z_start(d, g)

    zero_state = jnp.zeros((MODES, GROUP_CH), F32)
    state_row = lax.broadcasted_iota(jnp.int32, (states, GROUP_CH), 0) // MODES

    def entering(d, g):
        m = pl.ds(pl.multiple_of(g * MODES, MODES), MODES)
        for step in (1, 3, 2):
            arrived(sz, zrecv, d, g, lax.rem(z + step, NZ))
        x = xpart[g]
        for i in range(NZ):
            x = x + wts[3 * d + 2, i, m, :] * sz[d, i, g]
        full = jnp.where(state_row == g, jnp.concatenate([x] * groups, axis=0), 0.0)
        hi, lo = split(full)
        return jnp.concatenate([hi, lo, hi], axis=0)

    @pl.loop(0, groups)
    def _(g):
        load(1, g).wait()
        load(2, g).wait()
        for a in (0, 1, 2):
            xs[a, 0:8, :] = halo[a, :, cols(g)].astype(F32) * inner
        xs[0, 8:16, :] = xin[0, g, 0:16, :].astype(F32)[0:8]
        qs[g, 0:8, :] = causal(0, taps(0, g), 0, 8)
        for a in (1, 2):
            for lo in range(0, length, ROWS):
                xs[a, 8 + lo : 8 + lo + ROWS, :] = xin[a, g, lo : lo + ROWS, :].astype(F32)
        wk = taps(1, g)
        wv = taps(2, g)
        for lo in range(0, length, ROWS):
            kk = causal(1, wk, lo, ROWS)
            vv = causal(2, wv, lo, ROWS)
            ks[g, lo : lo + ROWS, :] = kk
            vs[g, lo : lo + ROWS, :] = vv
            pb[g, lo : lo + ROWS, :] = (kk * vv).astype(BF16)
        s = mm(tailf[g], pb[g])
        sy[0, y, g] = s[0:MODES] + s[MODES : 2 * MODES]
        y_start(0, g)

    @pl.loop(0, groups)
    def _(g):
        y_total(0, g)
        skip = skipin[pl.ds(g, 1), :]
        head = pb[g, 0:half, :]
        fw[g, 0:half, :] = mm(wf[g, :, half:length], head) + skip * head.astype(F32)
        fw[g, half:length, :] = mm(wf[g], pb[g]) + skip * pb[g, half:length, :].astype(F32)

    acc[...] = jnp.zeros_like(acc)

    @pl.loop(0, groups)
    def _(g):
        load(3, g).wait()
        state = entering(0, g)
        gain = gainin[pl.ds(g, 1), :]
        for lo in range(0, length, GROUP_CH):
            r = slice(lo, lo + GROUP_CH)
            f = fw[g, r, :] + mm(leadf[r, :], state)
            fw[g, r, :] = f
            gated = qs[g, r, :] * f
            acc[0, r, :] += gated * gated
            acc[1, r, :] += (xin[3, g, r, :].astype(F32) * gain) * gated

    sums = []
    for a in range(2):
        for lo in range(0, length, GROUP_CH):
            sums.append(jnp.sum(acc[a, lo : lo + GROUP_CH, :].T, axis=0, keepdims=True))
    cs[tp] = jnp.concatenate(sums, axis=0)

    def sums_copy(step):
        return pltpu.make_async_remote_copy(
            src_ref=cs.at[tp],
            dst_ref=cs.at[tp],
            send_sem=csend.at[step],
            recv_sem=crecv.at[tp],
            device_id=(me, lax.rem(tp + step, ntp)),
            device_id_type=MESH,
        )

    for step in range(1, ntp):
        sums_copy(step).start()
    for step in range(1, ntp):
        slot = lax.rem(tp + step, ntp)
        pltpu.make_async_copy(cs.at[slot], cs.at[slot], crecv.at[slot]).wait()
    total = cs[0]
    for i in range(1, ntp):
        total = total + cs[i]
    width = float(groups * GROUP_CH * ntp)
    blocks = length // GROUP_CH
    scale = lax.rsqrt(total[0:blocks] / width + EPSILON)
    cubed = scale * scale * scale * (total[blocks : 2 * blocks] / width)
    for b in range(blocks):
        r = slice(b * GROUP_CH, (b + 1) * GROUP_CH)
        scales[0, r, :] = jnp.broadcast_to(scale[b : b + 1, :], (GROUP_CH, GROUP_CH)).T
        scales[1, r, :] = jnp.broadcast_to(cubed[b : b + 1, :], (GROUP_CH, GROUP_CH)).T

    def edge_copy(a, g):
        return pltpu.make_async_remote_copy(
            src_ref=grads.at[a, g, pl.ds(0, 8), :],
            dst_ref=grads.at[a, g, pl.ds(length, 8), :],
            send_sem=gsend.at[a, g],
            recv_sem=grecv.at[a, g],
            device_id=(behind, tp),
            device_id_type=MESH,
        )

    def store(a, g):
        dst = (mixed_hbm, gq_hbm, gk_hbm, gv_hbm)[a]
        return pltpu.make_async_copy(outs.at[a, g], dst.at[:, cols(g)], out_sem.at[a, g])

    @pl.loop(0, groups)
    def _(g):
        gain = gainin[pl.ds(g, 1), :]
        for lo in range(0, length, ROWS):
            r = slice(lo, lo + ROWS)
            q = qs[g, r, :]
            f = fw[g, r, :]
            gated = q * f
            scale = scales[0, r, :]
            outs[0, g, r, :] = (gated * scale * gain).astype(BF16)
            d_gated = scale * (xin[3, g, r, :].astype(F32) * gain) - scales[1, r, :] * gated
            grads[0, g, r, :] = d_gated * f
            pb[g, r, :] = (d_gated * q).astype(BF16)
        s = mm(tailb[g], pb[g])
        sy[1, y, g] = s[0:MODES] + s[MODES : 2 * MODES]
        y_start(1, g)
        edge_copy(0, g).start()
        store(0, g).start()

    @pl.loop(0, groups)
    def _(g):
        y_total(1, g)
        skip = skipin[pl.ds(g, 1), :]
        rest = pb[g, half:length, :]
        fw[g, 0:half, :] = mm(wb[g], pb[g]) + skip * pb[g, 0:half, :].astype(F32)
        fw[g, half:length, :] = mm(wb[g, :, 0:half], rest) + skip * rest.astype(F32)

    def finish(a, g):
        edge_copy(a, g).wait_recv()
        grads[a, g, length : length + 8, :] = grads[a, g, length : length + 8, :] * final
        w = taps(a, g)
        for lo in range(0, length, ROWS):
            outs[a + 1, g, lo : lo + ROWS, :] = later(a, g, w, lo, ROWS).astype(BF16)
        store(a + 1, g).start()

    @pl.loop(0, groups)
    def _(g):
        finish(0, g)

    @pl.loop(0, groups)
    def _(g):
        state = entering(1, g)
        for lo in range(0, length, GROUP_CH):
            r = slice(lo, lo + GROUP_CH)
            dp = fw[g, r, :] + mm(leadb[r, :], state)
            grads[1, g, r, :] = dp * vs[g, r, :]
            grads[2, g, r, :] = dp * ks[g, r, :]
        edge_copy(1, g).start()
        edge_copy(2, g).start()

    @pl.loop(0, groups)
    def _(g):
        finish(1, g)
        finish(2, g)

    for a in range(3):
        halo_copy(a).wait_send()
    for step in range(1, ntp):
        sums_copy(step).wait_send()

    @pl.loop(0, groups)
    def _(g):
        for d in range(2):
            for step in range(1, NY):
                state_copy(sy, ysend, yrecv, y, d, g, step, ypeer(step)).wait_send()
            for step in range(1, NZ):
                state_copy(sz, zsend, zrecv, z, d, g, step, zpeer(step)).wait_send()
        for a in range(3):
            edge_copy(a, g).wait_send()
        for a in range(4):
            store(a, g).wait()


def body(q_in, k_in, v_in, short_weight, decay_rate, residue, skip, gain, d_out):
    length, channels = q_in.shape
    groups = channels // GROUP_CH
    ntp = lax.axis_size("tp")
    half = length // 2
    states = groups * MODES
    vmem = pltpu.VMEM
    dma = pltpu.SemaphoreType.DMA
    result = jax.ShapeDtypeStruct((length, channels), BF16)
    scratch = [
        vmem((4, groups, length, GROUP_CH), BF16),
        vmem(short_weight.shape, F32),
        vmem((groups, MODES), F32),
        vmem((groups, MODES), F32),
        vmem((groups, GROUP_CH), F32),
        vmem((groups, GROUP_CH), F32),
        vmem((3, 8, channels), BF16),
        vmem((3, length + 8, GROUP_CH), F32),
        vmem((groups, length, GROUP_CH), F32),
        vmem((groups, length, GROUP_CH), F32),
        vmem((groups, length, GROUP_CH), F32),
        vmem((groups, length, GROUP_CH), BF16),
        vmem((groups, length, GROUP_CH), F32),
        vmem((3, groups, length + 8, GROUP_CH), F32),
        vmem((4, groups, length, GROUP_CH), BF16),
        vmem((groups, half, length), BF16),
        vmem((groups, half, length), BF16),
        vmem((length, 3 * states), BF16),
        vmem((length, 3 * states), BF16),
        vmem((groups, 2 * MODES, length), BF16),
        vmem((groups, 2 * MODES, length), BF16),
        vmem((6, 4, states, GROUP_CH), F32),
        vmem((2, length, GROUP_CH), F32),
        vmem((2, length, GROUP_CH), F32),
        vmem((groups, MODES, GROUP_CH), F32),
        vmem((2, NY, groups, MODES, GROUP_CH), F32),
        vmem((2, NZ, groups, MODES, GROUP_CH), F32),
        vmem((ntp, 8, GROUP_CH), F32),
        dma((4, groups)),
        dma((5,)),
        dma((4, groups)),
        dma((3,)),
        dma((3,)),
        dma((2, NY, groups)),
        dma((2, NY, groups)),
        dma((2, NZ, groups)),
        dma((2, NZ, groups)),
        dma((ntp,)),
        dma((ntp,)),
        dma((3, groups)),
        dma((3, groups)),
    ]
    return pl.pallas_call(
        functools.partial(kernel, ntp),
        out_shape=(result,) * 4,
        in_specs=[pl.BlockSpec(memory_space=pl.ANY)] * 9,
        out_specs=(pl.BlockSpec(memory_space=pl.ANY),) * 4,
        scratch_shapes=scratch,
        compiler_params=pltpu.CompilerParams(
            collective_id=0, has_side_effects=True, vmem_limit_bytes=60 * 1024 * 1024
        ),
        name="hyena_block",
    )(
        q_in, k_in, v_in, d_out, short_weight, decay_rate, residue,
        skip.reshape(groups, GROUP_CH), gain.reshape(groups, GROUP_CH),
    )


def solution(mesh):
    in_specs = (
        P("ctx", "tp"),
        P("ctx", "tp"),
        P("ctx", "tp"),
        P(None, None, "tp"),
        P("tp", None),
        P("tp", None),
        P("tp"),
        P("tp"),
        P("ctx", "tp"),
    )
    out_specs = (P("ctx", "tp"), P("ctx", "tp"), P("ctx", "tp"), P("ctx", "tp"))
    return jax.shard_map(body, mesh=mesh, in_specs=in_specs, out_specs=out_specs, check_vma=False)
```

time: 340 us -> 54.8 us (0.16)
  the two profiles are of different devices: /device:TPU:22 before, /device:TPU:0 now
where the time goes in v1:
time: 54.8 us; the launch traced here: 54.5 us
  Pallas kernels  47.4 us (86%)
  local copies, waits for them, and re-layouts  6.53 us (12%)
  between operations  0.65 us (1%)
    pallas_call x1, Pallas kernels, body(): pl.pallas_call(functools.partial(kernel, ntp), out_shape=(result,) * 4, i...  47.4 us
    unnamed x10, local copies, waits for them, and re-layouts  6.53 us

profile of v1, /device:TPU:0, one launch (start us, length us, event | category | flops | bytes accessed | tf_op | source)
XLA Modules:
  0.0 54.5 jit_solution(11191453828022020916)
XLA Ops:
  0.6 47.4 %hyena_block.1 = (bf16[512,1024]{1,0:T(8,128)(2,1)}, bf16[512,1024]{1,0:T(8,128)(2,1)}, bf16[512,1024]{1,0:T(8,128)(2,1)}, bf16[512,1024]{1,0:T(8,128)(2,1)}) custom-call(bf16[512,1024]{1,0:T(8,128)(2,1)} %q_hbm.1, bf16[512,1024]{1,0:T(8,128)(2,1)} %k_hbm.1, bf16[512,1024]{1,0:T(8,128)(2,1)} %v_hbm.1, bf16[512,1024]{1,0:T(8,128)(2,1)} %d_hbm.1, ...), custom_call_target="tpu_custom_call" | custom-call | tf_op jit(solution)/shard_map/hyena_block/pallas_call | solution.py:502
  48.0 0.0 copy-start.2
  48.0 2.4 %copy.17 = bf16[512,1024]{1,0:T(8,128)(2,1)} copy(bf16[512,1024]{1,0:T(8,128)(2,1)} %get-tuple-element.8) | data formatting | bytes 2097152
  50.4 0.0 copy-done.2
  50.4 0.0 copy-start.1
  50.4 1.0 %copy.18 = bf16[512,1024]{1,0:T(8,128)(2,1)} copy(bf16[512,1024]{1,0:T(8,128)(2,1)S(1)} %copy-done.2) | data formatting | bytes 2097152
  51.3 0.6 %copy-done.1 = bf16[512,1024]{1,0:T(8,128)(2,1)S(1)} copy-done((bf16[512,1024]{1,0:T(8,128)(2,1)S(1)}, bf16[512,1024]{1,0:T(8,128)(2,1)}, u32[]{:S(2)}) %copy-start.1) | copy-done | bytes 1048600
  52.0 0.0 copy-start
  52.0 1.0 %copy.19 = bf16[512,1024]{1,0:T(8,128)(2,1)} copy(bf16[512,1024]{1,0:T(8,128)(2,1)S(1)} %copy-done.1) | data formatting | bytes 2097152
  52.9 0.6 %copy-done = bf16[512,1024]{1,0:T(8,128)(2,1)S(1)} copy-done((bf16[512,1024]{1,0:T(8,128)(2,1)S(1)}, bf16[512,1024]{1,0:T(8,128)(2,1)}, u32[]{:S(2)}) %copy-start) | copy-done | bytes 1048600
  53.6 1.0 %copy.20 = bf16[512,1024]{1,0:T(8,128)(2,1)} copy(bf16[512,1024]{1,0:T(8,128)(2,1)S(1)} %copy-done) | data formatting | bytes 2097152
Async XLA Ops:
  48.0 2.4 %copy-start.2 = (bf16[512,1024]{1,0:T(8,128)(2,1)S(1)}, bf16[512,1024]{1,0:T(8,128)(2,1)}, u32[]{:S(2)}) copy-start(bf16[512,1024]{1,0:T(8,128)(2,1)} %get-tuple-element.9) | copy-start | bytes 3145732
  50.4 1.6 %copy-start.1 = (bf16[512,1024]{1,0:T(8,128)(2,1)S(1)}, bf16[512,1024]{1,0:T(8,128)(2,1)}, u32[]{:S(2)}) copy-start(bf16[512,1024]{1,0:T(8,128)(2,1)} %get-tuple-element.10) | copy-start | bytes 3145732
  52.0 1.6 %copy-start = (bf16[512,1024]{1,0:T(8,128)(2,1)S(1)}, bf16[512,1024]{1,0:T(8,128)(2,1)}, u32[]{:S(2)}) copy-start(bf16[512,1024]{1,0:T(8,128)(2,1)} %get-tuple-element.11) | copy-start | bytes 3145732

commit v2 on v1

v2 whole, which is shorter than its diff:
```python
import functools

import jax
import jax.numpy as jnp
from jax import lax
from jax.experimental import pallas as pl
from jax.experimental.pallas import tpu as pltpu
from jax.sharding import PartitionSpec as P

KER = 7
MODES = 16
GROUP_CH = 128
EPSILON = 1e-05
NZ = 4
NY = 4
ROWS = 64
PAIR = 2
GRANT = 61_760_000
MESH = pl.DeviceIdType.MESH
F32 = jnp.float32
BF16 = jnp.bfloat16


def split(x):
    hi = x.astype(BF16)
    lo = (x - hi.astype(F32)).astype(BF16)
    return hi, lo


def mm(a, b):
    return jnp.dot(a, b, preferred_element_type=F32)


def cols(g):
    return pl.ds(pl.multiple_of(g * GROUP_CH, GROUP_CH), GROUP_CH)


def later(src, g, w, lo, rows):
    total = w[0] * src[g, pl.ds(lo, rows), :]
    for j in range(1, KER):
        total = total + w[j] * src[g, pl.ds(lo + j, rows), :]
    return total


def main_kernel(
    ntp,
    q_hbm, k_hbm, v_hbm, d_hbm, w_hbm, rate_hbm, res_hbm, skip_hbm, gain_hbm,
    mixed, gq, gk, dv,
    xin, win, ratein, resin, skipin, gainin,
    halo, xs, qs, ks, vs, pb, fw, dq, dk, edge,
    wf, wb, af, ab, tailf, tailb, ratew, rate3, coef3, dec, far,
    acc, scales, xpart, sy, sz, cs,
    in_sem, par_sem,
    hsend, hrecv, ysend, yrecv, zsend, zrecv, csend, crecv, gsend, grecv,
):
    length = xin.shape[1]
    groups = xin.shape[2] // GROUP_CH
    pairs = groups // PAIR
    states = groups * MODES
    blocks = length // GROUP_CH
    nctx = NZ * NY
    me = lax.axis_index("ctx")
    tp = lax.axis_index("tp")
    z = lax.div(me, NY)
    y = lax.rem(me, NY)
    behind = lax.rem(me + nctx - 1, nctx)
    ahead = lax.rem(me + 1, nctx)

    params = [
        pltpu.make_async_copy(src, dst, par_sem.at[i])
        for i, (src, dst) in enumerate(
            ((rate_hbm, ratein), (res_hbm, resin), (w_hbm, win), (skip_hbm, skipin), (gain_hbm, gainin))
        )
    ]
    for copy in params:
        copy.start()

    def load(a):
        return pltpu.make_async_copy((q_hbm, k_hbm, v_hbm, d_hbm)[a], xin.at[a], in_sem.at[a])

    for a in (1, 2, 0, 3):
        load(a).start()

    bar = pltpu.get_barrier_semaphore()

    def greet(c, t):
        pl.semaphore_signal(bar, inc=1, device_id=(c, t), device_id_type=MESH)

    def ypeer(step):
        return z * NY + lax.rem(y + step, NY)

    def zpeer(step):
        return lax.rem(z + step, NZ) * NY + y

    greet(behind, tp)
    greet(ahead, tp)
    for step in range(1, NY):
        greet(ypeer(step), tp)
    for step in range(1, NZ):
        greet(zpeer(step), tp)
    for step in range(1, ntp):
        greet(me, lax.rem(tp + step, ntp))

    for copy in params:
        copy.wait()

    rate = ratein[...]
    r2 = rate * rate
    sinhc = 1.0 + r2 * (1 / 6) * (1.0 + r2 * (1 / 20) * (1.0 + r2 * (1 / 42) * (1.0 + r2 * (1 / 72) * (1.0 + r2 * (1 / 110)))))
    coef = resin[...] * jnp.sqrt(2.0 * rate * jnp.exp(-rate) * sinhc)
    rate3[...] = jnp.concatenate([rate] * 3, axis=1)
    coef3[...] = jnp.concatenate([coef] * 3, axis=1)
    row_i = lax.broadcasted_iota(jnp.int32, (MODES, MODES), 0)
    col_i = lax.broadcasted_iota(jnp.int32, (MODES, MODES), 1)
    yf = y.astype(F32)
    for g in range(groups):
        m = slice(g * MODES, (g + 1) * MODES)
        column = jnp.sum(
            jnp.where(row_i == col_i, jnp.broadcast_to(rate[g : g + 1, :], (MODES, MODES)), 0.0), axis=1, keepdims=True
        )
        wide = jnp.broadcast_to(column, (MODES, GROUP_CH))
        ratew[m, :] = wide
        for i in range(blocks):
            dec[i, m, :] = jnp.exp(wide * (-1.0 * GROUP_CH * (i + 1)))
        far[0, m, :] = jnp.exp(wide * (-float(length) * yf))
        far[1, m, :] = jnp.exp(wide * (-float(length) * (NY - 1.0 - yf)))
        far[2, m, :] = jnp.exp(wide * (-float(length) * NY))

    i_idx = lax.broadcasted_iota(jnp.int32, (GROUP_CH, 3 * MODES), 0).astype(F32)
    first = lax.broadcasted_iota(jnp.int32, (GROUP_CH, 3 * MODES), 1) < 2 * MODES
    lag = lax.broadcasted_iota(jnp.int32, (MODES, GROUP_CH), 1).astype(F32)
    ti = lax.broadcasted_iota(jnp.int32, (GROUP_CH, GROUP_CH), 0)
    tj = lax.broadcasted_iota(jnp.int32, (GROUP_CH, GROUP_CH), 1)

    @pl.loop(0, pairs)
    def _(p):
        for e in range(PAIR):
            g = p * PAIR + e
            r_row = rate3[pl.ds(g, 1), :]
            c_row = coef3[pl.ds(g, 1), :]
            for a, expo in ((af, float(GROUP_CH - 1) - i_idx), (ab, i_idx)):
                x = c_row * jnp.exp(r_row * expo)
                hi = x.astype(BF16).astype(F32)
                a[g] = jnp.where(first, hi, x - hi).astype(BF16)
            wide = ratew[pl.ds(pl.multiple_of(g * MODES, MODES), MODES), :]
            for b in range(blocks):
                at = lag + float(b * GROUP_CH)
                c = slice(b * GROUP_CH, (b + 1) * GROUP_CH)
                for tail, expo in ((tailf, float(length - 1) - at), (tailb, at)):
                    hi, lo = split(jnp.exp(-wide * expo))
                    tail[g, 0:MODES, c] = hi
                    tail[g, MODES : 2 * MODES, c] = lo
                    tail[g, 2 * MODES : 3 * MODES, c] = hi
        for e in range(PAIR):
            g = p * PAIR + e
            for b in range(blocks):
                c = slice(b * GROUP_CH, (b + 1) * GROUP_CH)
                w = mm(af[g], tailf[g, :, c])
                if b == blocks - 1:
                    w = jnp.where(ti >= tj, w, 0.0)
                w = w.astype(BF16)
                wf[g, :, c] = w
                w = mm(ab[g], tailb[g, :, c])
                if b == 0:
                    w = jnp.where(tj >= ti, w, 0.0)
                w = w.astype(BF16)
                wb[g, :, c] = w

    pl.semaphore_wait(bar, 2 + NY - 1 + NZ - 1 + ntp - 1)

    def halo_copy(a):
        src = (q_hbm, k_hbm, v_hbm)[a]
        return pltpu.make_async_remote_copy(
            src_ref=src.at[pl.ds(length - 8, 8), :],
            dst_ref=halo.at[a],
            send_sem=hsend.at[a],
            recv_sem=hrecv.at[a],
            device_id=(ahead, tp),
            device_id_type=MESH,
        )

    for a in (1, 2, 0):
        halo_copy(a).start()

    inner = (me > 0).astype(F32)
    final = (me < nctx - 1).astype(F32)

    def taps(a, g):
        return [win[a, j : j + 1, cols(g)] for j in range(KER)]

    def stage(slot, a, g):
        xs[slot, 0:8, :] = halo[a, :, cols(g)].astype(F32) * inner
        for lo in range(0, length, ROWS):
            xs[slot, 8 + lo : 8 + lo + ROWS, :] = xin[a, lo : lo + ROWS, cols(g)].astype(F32)

    def causal(slot, w, lo, rows):
        total = w[0] * xs[slot, pl.ds(8 + lo, rows), :]
        for j in range(1, KER):
            total = total + w[j] * xs[slot, pl.ds(8 + lo - j, rows), :]
        return total

    def state_copy(buf, send, recv, mine, d, p, step, peer):
        return pltpu.make_async_remote_copy(
            src_ref=buf.at[d, mine, p],
            dst_ref=buf.at[d, mine, p],
            send_sem=send.at[d, step, p],
            recv_sem=recv.at[d, mine, p],
            device_id=(peer, tp),
            device_id_type=MESH,
        )

    def y_start(d, p):
        for step in (1, 3, 2):
            state_copy(sy, ysend, yrecv, y, d, p, step, ypeer(step)).start()

    def z_start(d, p):
        for step in (1, 3, 2):
            state_copy(sz, zsend, zrecv, z, d, p, step, zpeer(step)).start()

    def arrived(buf, recv, d, p, slot):
        pltpu.make_async_copy(buf.at[d, slot, p], buf.at[d, slot, p], recv.at[d, slot, p]).wait()

    def modes(g):
        return pl.ds(pl.multiple_of(g * MODES, MODES), MODES)

    def y_total(d, p):
        for step in (1, 3, 2):
            arrived(sy, yrecv, d, p, lax.rem(y + step, NY))
        for e in range(PAIR):
            g = p * PAIR + e
            decay = dec[blocks - 1, modes(g), :]
            part = jnp.zeros((MODES, GROUP_CH), F32)
            total = jnp.zeros((MODES, GROUP_CH), F32)
            for i in range(NY) if d == 0 else reversed(range(NY)):
                s = sy[d, i, p, e]
                before = (i < y) if d == 0 else (i > y)
                part = jnp.where(before, decay * part + s, part)
                total = decay * total + s
            xpart[p, e] = part
            sz[d, z, p, e] = total
        z_start(d, p)

    def z_wait(d, p):
        for step in (1, 3, 2):
            arrived(sz, zrecv, d, p, lax.rem(z + step, NZ))

    def entering(d, p, e):
        m = modes(p * PAIR + e)
        decay = far[2, m, :]
        total = jnp.zeros((MODES, GROUP_CH), F32)
        for i in range(NZ) if d == 0 else reversed(range(NZ)):
            before = (i < z) if d == 0 else (i > z)
            total = jnp.where(before, decay * total + sz[d, i, p, e], total)
        x = xpart[p, e] + far[d, m, :] * total
        parts = []
        for b in range(blocks):
            hi, lo = split(x * dec[b if d == 0 else blocks - 1 - b, m, :])
            parts.append(jnp.concatenate([hi, lo, hi], axis=0))
        return parts

    for a in (1, 2, 0):
        halo_copy(a).wait_recv()
    for a in range(3):
        load(a).wait()

    @pl.loop(0, pairs)
    def _(p):
        for e in range(PAIR):
            g = p * PAIR + e
            stage(2 * e, 1, g)
            stage(2 * e + 1, 2, g)
            wk = taps(1, g)
            wv = taps(2, g)
            for lo in range(0, length, ROWS):
                kk = causal(2 * e, wk, lo, ROWS)
                vv = causal(2 * e + 1, wv, lo, ROWS)
                ks[g, lo : lo + ROWS, :] = kk
                vs[g, lo : lo + ROWS, :] = vv
                pb[g, lo : lo + ROWS, :] = (kk * vv).astype(BF16)
            s = mm(tailf[g, 0 : 2 * MODES], pb[g])
            sy[0, y, p, e] = s[0:MODES] + s[MODES : 2 * MODES]
        y_start(0, p)

    @pl.loop(0, pairs)
    def _(p):
        y_total(0, p)
        for e in range(PAIR):
            g = p * PAIR + e
            stage(e, 0, g)
            w = taps(0, g)
            skip = skipin[pl.ds(g, 1), :]
            for b in range(blocks):
                r = slice(b * GROUP_CH, (b + 1) * GROUP_CH)
                here = mm(wf[g, :, (blocks - 1 - b) * GROUP_CH :], pb[g, 0 : (b + 1) * GROUP_CH, :])
                for lo in range(b * GROUP_CH, (b + 1) * GROUP_CH, ROWS):
                    qs[g, lo : lo + ROWS, :] = causal(e, w, lo, ROWS)
                fw[g, r, :] = here + skip * pb[g, r, :].astype(F32)

    acc[...] = jnp.zeros_like(acc)
    load(3).wait()

    @pl.loop(0, pairs)
    def _(p):
        z_wait(0, p)
        states_in = [entering(0, p, e) for e in range(PAIR)]
        for b in range(blocks):
            r = slice(b * GROUP_CH, (b + 1) * GROUP_CH)
            squares = acc[0, r, :]
            aligned = acc[1, r, :]
            for e in range(PAIR):
                g = p * PAIR + e
                gain = gainin[pl.ds(g, 1), :]
                f = fw[g, r, :] + mm(af[g], states_in[e][b])
                fw[g, r, :] = f
                gated = qs[g, r, :] * f
                squares = squares + gated * gated
                aligned = aligned + (xin[3, r, cols(g)].astype(F32) * gain) * gated
            acc[0, r, :] = squares
            acc[1, r, :] = aligned

    sums = []
    for a in range(2):
        for lo in range(0, length, GROUP_CH):
            sums.append(jnp.sum(acc[a, lo : lo + GROUP_CH, :].T, axis=0, keepdims=True))
    cs[tp] = jnp.concatenate(sums, axis=0)

    def sums_copy(step):
        return pltpu.make_async_remote_copy(
            src_ref=cs.at[tp],
            dst_ref=cs.at[tp],
            send_sem=csend.at[step],
            recv_sem=crecv.at[tp],
            device_id=(me, lax.rem(tp + step, ntp)),
            device_id_type=MESH,
        )

    for step in range(1, ntp):
        sums_copy(step).start()
    for step in range(1, ntp):
        slot = lax.rem(tp + step, ntp)
        pltpu.make_async_copy(cs.at[slot], cs.at[slot], crecv.at[slot]).wait()
    total = cs[0]
    for i in range(1, ntp):
        total = total + cs[i]
    width = float(groups * GROUP_CH * ntp)
    scale = lax.rsqrt(total[0:blocks] / width + EPSILON)
    cubed = scale * scale * scale * (total[blocks : 2 * blocks] / width)
    for b in range(blocks):
        r = slice(b * GROUP_CH, (b + 1) * GROUP_CH)
        scales[0, r, :] = jnp.broadcast_to(scale[b : b + 1, :], (GROUP_CH, GROUP_CH)).T
        scales[1, r, :] = jnp.broadcast_to(cubed[b : b + 1, :], (GROUP_CH, GROUP_CH)).T

    def edge_copy(a, g):
        return pltpu.make_async_remote_copy(
            src_ref=(dq, dk, dv)[a].at[g, pl.ds(0, 8), :],
            dst_ref=edge.at[a, g],
            send_sem=gsend.at[a, g],
            recv_sem=grecv.at[a, g],
            device_id=(behind, tp),
            device_id_type=MESH,
        )

    @pl.loop(0, pairs)
    def _(p):
        for e in range(PAIR):
            g = p * PAIR + e
            gain = gainin[pl.ds(g, 1), :]
            for lo in range(0, length, ROWS):
                r = slice(lo, lo + ROWS)
                q = qs[g, r, :]
                f = fw[g, r, :]
                gated = q * f
                scale = scales[0, r, :]
                mixed[r, cols(g)] = (gated * scale * gain).astype(BF16)
                d_gated = scale * (xin[3, r, cols(g)].astype(F32) * gain) - scales[1, r, :] * gated
                dq[g, r, :] = d_gated * f
                pb[g, r, :] = (d_gated * q).astype(BF16)
            s = mm(tailb[g, 0 : 2 * MODES], pb[g])
            sy[1, y, p, e] = s[0:MODES] + s[MODES : 2 * MODES]
        y_start(1, p)
        for e in range(PAIR):
            edge_copy(0, p * PAIR + e).start()

    def attach(a, g):
        edge_copy(a, g).wait_recv()
        (dq, dk, dv)[a][g, length : length + 8, :] = edge[a, g] * final

    @pl.loop(0, pairs)
    def _(p):
        y_total(1, p)
        for e in range(PAIR):
            attach(0, p * PAIR + e)
        for e in range(PAIR):
            g = p * PAIR + e
            w = taps(0, g)
            skip = skipin[pl.ds(g, 1), :]
            for b in range(blocks):
                r = slice(b * GROUP_CH, (b + 1) * GROUP_CH)
                here = mm(wb[g, :, 0 : (blocks - b) * GROUP_CH], pb[g, b * GROUP_CH :, :])
                for lo in range(b * GROUP_CH, (b + 1) * GROUP_CH, ROWS):
                    gq[lo : lo + ROWS, cols(g)] = later(dq, g, w, lo, ROWS).astype(BF16)
                fw[g, r, :] = here + skip * pb[g, r, :].astype(F32)

    @pl.loop(0, pairs)
    def _(p):
        z_wait(1, p)
        states_in = [entering(1, p, e) for e in range(PAIR)]
        for e in range(PAIR):
            g = p * PAIR + e
            for b in range(blocks):
                r = slice(b * GROUP_CH, (b + 1) * GROUP_CH)
                dp = fw[g, r, :] + mm(ab[g], states_in[e][b])
                dk[g, r, :] = dp * vs[g, r, :]
                dv[g, r, :] = dp * ks[g, r, :]
        for e in range(PAIR):
            edge_copy(1, p * PAIR + e).start()
            edge_copy(2, p * PAIR + e).start()

    @pl.loop(0, pairs)
    def _(p):
        for e in range(PAIR):
            attach(1, p * PAIR + e)
        for e in range(PAIR):
            g = p * PAIR + e
            w = taps(1, g)
            for lo in range(0, length, ROWS):
                gk[lo : lo + ROWS, cols(g)] = later(dk, g, w, lo, ROWS).astype(BF16)

    for a in range(3):
        halo_copy(a).wait_send()
    for step in range(1, ntp):
        sums_copy(step).wait_send()

    @pl.loop(0, pairs)
    def _(p):
        for d in range(2):
            for step in range(1, NY):
                state_copy(sy, ysend, yrecv, y, d, p, step, ypeer(step)).wait_send()
            for step in range(1, NZ):
                state_copy(sz, zsend, zrecv, z, d, p, step, zpeer(step)).wait_send()
        for e in range(PAIR):
            for a in range(3):
                edge_copy(a, p * PAIR + e).wait_send()
            attach(2, p * PAIR + e)


def tail_kernel(mixed, gq, gk, dv, w_hbm, mixed_hbm, gq_hbm, gk_hbm, gv_hbm, win, out, sem, out_sem):
    groups, length = dv.shape[0], out.shape[1]
    taps_in = pltpu.make_async_copy(w_hbm.at[2], win, sem.at[0])
    taps_in.start()
    whole = [
        pltpu.make_async_copy(src, dst, sem.at[1 + i])
        for i, (src, dst) in enumerate(((mixed, mixed_hbm), (gq, gq_hbm), (gk, gk_hbm)))
    ]
    for copy in whole:
        copy.start()
    taps_in.wait()

    def store(g):
        return pltpu.make_async_copy(out.at[g], gv_hbm.at[:, cols(g)], out_sem.at[g])

    @pl.loop(0, groups)
    def _(g):
        w = [win[j : j + 1, cols(g)] for j in range(KER)]
        for lo in range(0, length, ROWS):
            out[g, lo : lo + ROWS, :] = later(dv, g, w, lo, ROWS).astype(BF16)
        store(g).start()

    for copy in whole:
        copy.wait()

    @pl.loop(0, groups)
    def _(g):
        store(g).wait()


def body(q_in, k_in, v_in, short_weight, decay_rate, residue, skip, gain, d_out):
    length, channels = q_in.shape
    groups = channels // GROUP_CH
    pairs = groups // PAIR
    ntp = lax.axis_size("tp")
    states = groups * MODES
    blocks = length // GROUP_CH
    vmem = pltpu.VMEM
    dma = pltpu.SemaphoreType.DMA
    here = pl.BlockSpec(memory_space=pltpu.VMEM)
    anywhere = pl.BlockSpec(memory_space=pl.ANY)
    scratch = [
        vmem((4, length, channels), BF16),
        vmem(short_weight.shape, F32),
        vmem((groups, MODES), F32),
        vmem((groups, MODES), F32),
        vmem((groups, GROUP_CH), F32),
        vmem((groups, GROUP_CH), F32),
        vmem((3, 8, channels), BF16),
        vmem((4, length + 8, GROUP_CH), F32),
        vmem((groups, length, GROUP_CH), F32),
        vmem((groups, length, GROUP_CH), F32),
        vmem((groups, length, GROUP_CH), F32),
        vmem((groups, length, GROUP_CH), BF16),
        vmem((groups, length, GROUP_CH), F32),
        vmem((groups, length + 8, GROUP_CH), F32),
        vmem((groups, length + 8, GROUP_CH), F32),
        vmem((3, groups, 8, GROUP_CH), F32),
        vmem((groups, GROUP_CH, length), BF16),
        vmem((groups, GROUP_CH, length), BF16),
        vmem((groups, GROUP_CH, 3 * MODES), BF16),
        vmem((groups, GROUP_CH, 3 * MODES), BF16),
        vmem((groups, 3 * MODES, length), BF16),
        vmem((groups, 3 * MODES, length), BF16),
        vmem((states, GROUP_CH), F32),
        vmem((groups, 3 * MODES), F32),
        vmem((groups, 3 * MODES), F32),
        vmem((blocks, states, GROUP_CH), F32),
        vmem((3, states, GROUP_CH), F32),
        vmem((2, length, GROUP_CH), F32),
        vmem((2, length, GROUP_CH), F32),
        vmem((pairs, PAIR, MODES, GROUP_CH), F32),
        vmem((2, NY, pairs, PAIR, MODES, GROUP_CH), F32),
        vmem((2, NZ, pairs, PAIR, MODES, GROUP_CH), F32),
        vmem((ntp, 8, GROUP_CH), F32),
        dma((4,)),
        dma((5,)),
        dma((3,)),
        dma((3,)),
        dma((2, NY, pairs)),
        dma((2, NY, pairs)),
        dma((2, NZ, pairs)),
        dma((2, NZ, pairs)),
        dma((ntp,)),
        dma((ntp,)),
        dma((3, groups)),
        dma((3, groups)),
    ]
    mixed, gq, gk, dv = pl.pallas_call(
        functools.partial(main_kernel, ntp),
        out_shape=(
            vmem((length, channels), BF16),
            vmem((length, channels), BF16),
            vmem((length, channels), BF16),
            vmem((groups, length + 8, GROUP_CH), F32),
        ),
        in_specs=[anywhere] * 9,
        out_specs=(here,) * 4,
        scratch_shapes=scratch,
        compiler_params=pltpu.CompilerParams(
            collective_id=0, has_side_effects=True, vmem_limit_bytes=GRANT
        ),
        name="hyena_main",
    )(
        q_in, k_in, v_in, d_out, short_weight, decay_rate, residue,
        skip.reshape(groups, GROUP_CH), gain.reshape(groups, GROUP_CH),
    )
    result = jax.ShapeDtypeStruct((length, channels), BF16)
    return pl.pallas_call(
        tail_kernel,
        out_shape=(result,) * 4,
        in_specs=[here] * 4 + [anywhere],
        out_specs=(anywhere,) * 4,
        scratch_shapes=[
            vmem(short_weight.shape[1:], F32),
            vmem((groups, length, GROUP_CH), BF16),
            dma((4,)),
            dma((groups,)),
        ],
        compiler_params=pltpu.CompilerParams(vmem_limit_bytes=8 * 1024 * 1024),
        name="hyena_tail",
    )(mixed, gq, gk, dv, short_weight)


def solution(mesh):
    in_specs = (
        P("ctx", "tp"),
        P("ctx", "tp"),
        P("ctx", "tp"),
        P(None, None, "tp"),
        P("tp", None),
        P("tp", None),
        P("tp"),
        P("tp"),
        P("ctx", "tp"),
    )
    out_specs = (P("ctx", "tp"), P("ctx", "tp"), P("ctx", "tp"), P("ctx", "tp"))
    return jax.shard_map(body, mesh=mesh, in_specs=in_specs, out_specs=out_specs, check_vma=False)
```

time: 54.8 us -> 46.8 us (0.85)
  local copies, waits for them, and re-layouts: 6.53 us -> 0.89 us
  Pallas kernels: 47.4 us -> 45.1 us
    unnamed x10 -> x2, local copies, waits for them, and re-layouts: 6.53 us -> 0.89 us
    pallas_call x1 -> x2, Pallas kernels: 47.4 us -> 45.1 us  [the longest x1 43 us: body(): pl.pallas_call(functools.partial(main_kernel, ntp), out_shape=(vmem((leng...]
where the time goes in v2:
time: 46.8 us; the launch traced here: 46.7 us
  Pallas kernels  45.1 us (96%)
  local copies, waits for them, and re-layouts  0.89 us (2%)
  between operations  0.65 us (1%)
    pallas_call x1, Pallas kernels, body(): pl.pallas_call(functools.partial(main_kernel, ntp), out_shape=(vmem((leng...  43 us
    pallas_call x1, Pallas kernels, body(): pl.pallas_call(tail_kernel, out_shape=(result,) * 4, in_specs=[here] * 4...  2.1 us

profile of v2, /device:TPU:0, one launch (start us, length us, event | category | flops | bytes accessed | tf_op | source)
XLA Modules:
  0.0 46.7 jit_solution(15374585547117961908)
XLA Ops:
  0.6 43.0 %hyena_main.1 = (bf16[512,1024]{1,0:T(8,128)(2,1)S(1)}, bf16[512,1024]{1,0:T(8,128)(2,1)S(1)}, bf16[512,1024]{1,0:T(8,128)(2,1)S(1)}, f32[8,520,128]{2,1,0:T(8,128)S(1)}) custom-call(bf16[512,1024]{1,0:T(8,128)(2,1)} %q_hbm.1, bf16[512,1024]{1,0:T(8,128)(2,1)} %k_hbm.1, bf16[512,1024]{1,0:T(8,128)(2,1)} %v_hbm.1, bf16[512,1024]{1,0:T(8,128)(2,1)} %d_hbm.1, ...), custom_call_target="tpu_custom_call" | custom-call | tf_op jit(solution)/shard_map/hyena_main/pallas_call | solution.py:535
  43.7 0.0 copy-start
  43.7 0.9 %copy-done = f32[3,7,1024]{2,1,0:T(8,128)S(1)} copy-done((f32[3,7,1024]{2,1,0:T(8,128)S(1)}, f32[3,7,1024]{2,1,0:T(8,128)}, u32[]{:S(2)}) %copy-start) | copy-done | bytes 86040
  44.6 2.1 %hyena_tail.1 = (bf16[512,1024]{1,0:T(8,128)(2,1)}, bf16[512,1024]{1,0:T(8,128)(2,1)}, bf16[512,1024]{1,0:T(8,128)(2,1)}, bf16[512,1024]{1,0:T(8,128)(2,1)}) custom-call(bf16[512,1024]{1,0:T(8,128)(2,1)S(1)} %get-tuple-element.8.mixed, bf16[512,1024]{1,0:T(8,128)(2,1)S(1)} %get-tuple-element.9.gq, bf16[512,1024]{1,0:T(8,128)(2,1)S(1)} %get-tuple-element.10.gk, ...), custom_call_target="tpu_custom_call" | custom-call | tf_op jit(solution)/shard_map/hyena_tail/pallas_call | solution.py:555
Async XLA Ops:
  43.7 0.9 %copy-start = (f32[3,7,1024]{2,1,0:T(8,128)S(1)}, f32[3,7,1024]{2,1,0:T(8,128)}, u32[]{:S(2)}) copy-start(f32[3,7,1024]{2,1,0:T(8,128)} %w_hbm.3) | copy-start | bytes 258052

commit v3 on v2

--- a/solution.py
+++ b/solution.py
@@ -15,7 +15,7 @@
 NY = 4
 ROWS = 64
 PAIR = 2
-GRANT = 61_760_000
+GRANT = 61_720_000
 MESH = pl.DeviceIdType.MESH
 F32 = jnp.float32
 BF16 = jnp.bfloat16
@@ -45,13 +45,13 @@
 def main_kernel(
     ntp,
     q_hbm, k_hbm, v_hbm, d_hbm, w_hbm, rate_hbm, res_hbm, skip_hbm, gain_hbm,
-    mixed, gq, gk, dv,
+    mixed, gq, gk, dv, wtail,
     xin, win, ratein, resin, skipin, gainin,
-    halo, xs, qs, ks, vs, pb, fw, dq, dk, edge,
-    wf, wb, af, ab, tailf, tailb, ratew, rate3, coef3, dec, far,
+    halo, xs, lead, qs, ks, vs, pb, fw, dq, dk, eout, edge, before_k, before_v,
+    wf, wb, af, ab, tailf, tailb, hneg, ratew, rate3, coef3, dec, far,
     acc, scales, xpart, sy, sz, cs,
     in_sem, par_sem,
-    hsend, hrecv, ysend, yrecv, zsend, zrecv, csend, crecv, gsend, grecv,
+    hsend, hrecv, ysend, yrecv, zsend, zrecv, csend, crecv, gsend, grecv, bsend, brecv,
 ):
     length = xin.shape[1]
     groups = xin.shape[2] // GROUP_CH
@@ -69,7 +69,7 @@
     params = [
         pltpu.make_async_copy(src, dst, par_sem.at[i])
         for i, (src, dst) in enumerate(
-            ((rate_hbm, ratein), (res_hbm, resin), (w_hbm, win), (skip_hbm, skipin), (gain_hbm, gainin))
+            ((rate_hbm, ratein), (res_hbm, resin), (w_hbm, win), (skip_hbm, skipin), (gain_hbm, gainin), (w_hbm.at[2], wtail))
         )
     ]
     for copy in params:
@@ -100,6 +100,22 @@
         greet(zpeer(step), tp)
     for step in range(1, ntp):
         greet(me, lax.rem(tp + step, ntp))
+
+    pl.semaphore_wait(bar, 2 + NY - 1 + NZ - 1 + ntp - 1)
+
+    def halo_copy(a):
+        src = (q_hbm, k_hbm, v_hbm)[a]
+        return pltpu.make_async_remote_copy(
+            src_ref=src.at[pl.ds(length - 8, 8), :],
+            dst_ref=halo.at[a],
+            send_sem=hsend.at[a],
+            recv_sem=hrecv.at[a],
+            device_id=(ahead, tp),
+            device_id_type=MESH,
+        )
+
+    for a in (1, 2, 0):
+        halo_copy(a).start()
 
     for copy in params:
         copy.wait()
@@ -132,55 +148,37 @@
     ti = lax.broadcasted_iota(jnp.int32, (GROUP_CH, GROUP_CH), 0)
     tj = lax.broadcasted_iota(jnp.int32, (GROUP_CH, GROUP_CH), 1)
 
-    @pl.loop(0, pairs)
-    def _(p):
-        for e in range(PAIR):
-            g = p * PAIR + e
-            r_row = rate3[pl.ds(g, 1), :]
-            c_row = coef3[pl.ds(g, 1), :]
-            for a, expo in ((af, float(GROUP_CH - 1) - i_idx), (ab, i_idx)):
-                x = c_row * jnp.exp(r_row * expo)
+    def tables(d):
+        grow, tail, table = ((af, tailf, wf), (ab, tailb, wb))[d]
+
+        @pl.loop(0, pairs)
+        def _(p):
+            for e in range(PAIR):
+                g = p * PAIR + e
+                x = coef3[pl.ds(g, 1), :] * jnp.exp(rate3[pl.ds(g, 1), :] * (i_idx if d else float(GROUP_CH - 1) - i_idx))
                 hi = x.astype(BF16).astype(F32)
-                a[g] = jnp.where(first, hi, x - hi).astype(BF16)
-            wide = ratew[pl.ds(pl.multiple_of(g * MODES, MODES), MODES), :]
-            for b in range(blocks):
-                at = lag + float(b * GROUP_CH)
-                c = slice(b * GROUP_CH, (b + 1) * GROUP_CH)
-                for tail, expo in ((tailf, float(length - 1) - at), (tailb, at)):
-                    hi, lo = split(jnp.exp(-wide * expo))
+                grow[g] = jnp.where(first, hi, x - hi).astype(BF16)
+                wide = ratew[pl.ds(pl.multiple_of(g * MODES, MODES), MODES), :]
+                for b in range(blocks):
+                    at = lag + float(b * GROUP_CH)
+                    c = slice(b * GROUP_CH, (b + 1) * GROUP_CH)
+                    hi, lo = split(jnp.exp(-wide * (at if d else float(length - 1) - at)))
                     tail[g, 0:MODES, c] = hi
                     tail[g, MODES : 2 * MODES, c] = lo
                     tail[g, 2 * MODES : 3 * MODES, c] = hi
-        for e in range(PAIR):
-            g = p * PAIR + e
-            for b in range(blocks):
-                c = slice(b * GROUP_CH, (b + 1) * GROUP_CH)
-                w = mm(af[g], tailf[g, :, c])
-                if b == blocks - 1:
-                    w = jnp.where(ti >= tj, w, 0.0)
-                w = w.astype(BF16)
-                wf[g, :, c] = w
-                w = mm(ab[g], tailb[g, :, c])
-                if b == 0:
-                    w = jnp.where(tj >= ti, w, 0.0)
-                w = w.astype(BF16)
-                wb[g, :, c] = w
-
-    pl.semaphore_wait(bar, 2 + NY - 1 + NZ - 1 + ntp - 1)
-
-    def halo_copy(a):
-        src = (q_hbm, k_hbm, v_hbm)[a]
-        return pltpu.make_async_remote_copy(
-            src_ref=src.at[pl.ds(length - 8, 8), :],
-            dst_ref=halo.at[a],
-            send_sem=hsend.at[a],
-            recv_sem=hrecv.at[a],
-            device_id=(ahead, tp),
-            device_id_type=MESH,
-        )
-
-    for a in (1, 2, 0):
-        halo_copy(a).start()
+            for e in range(PAIR):
+                g = p * PAIR + e
+                for b in range(blocks):
+                    c = slice(b * GROUP_CH, (b + 1) * GROUP_CH)
+                    w = mm(grow[g], tail[g, :, c])
+                    if d == 1 and b == 0:
+                        hneg[g] = jnp.where(ti[0:8, 0:8] > tj[0:8, 0:8], w[0:8, 0:8], 0.0).astype(BF16)
+                        w = jnp.where(tj >= ti, w, 0.0)
+                    if d == 0 and b == blocks - 1:
+                        w = jnp.where(ti >= tj, w, 0.0)
+                    table[g, :, c] = w.astype(BF16)
+
+    tables(0)
 
     inner = (me > 0).astype(F32)
     final = (me < nctx - 1).astype(F32)
@@ -253,47 +251,94 @@
             total = jnp.where(before, decay * total + sz[d, i, p, e], total)
         x = xpart[p, e] + far[d, m, :] * total
         parts = []
+        if d == 1:
+            hi, lo = split(x)
+            parts.append(jnp.concatenate([hi, lo, hi], axis=0))
         for b in range(blocks):
             hi, lo = split(x * dec[b if d == 0 else blocks - 1 - b, m, :])
             parts.append(jnp.concatenate([hi, lo, hi], axis=0))
         return parts
 
-    for a in (1, 2, 0):
-        halo_copy(a).wait_recv()
-    for a in range(3):
+    def lead_rows(a, g, w):
+        total = w[0] * lead[a, g, 8:16, :]
+        for j in range(1, KER):
+            total = total + w[j] * lead[a, g, 8 - j : 16 - j, :]
+        return total
+
+    for a in (1, 2):
         load(a).wait()
 
     @pl.loop(0, pairs)
     def _(p):
         for e in range(PAIR):
             g = p * PAIR + e
-            stage(2 * e, 1, g)
-            stage(2 * e + 1, 2, g)
+            for a in (1, 2):
+                for lo in range(0, length, ROWS):
+                    xs[2 * e + a - 1, 8 + lo : 8 + lo + ROWS, :] = xin[a, lo : lo + ROWS, cols(g)].astype(F32)
+                lead[a, g, 8:16, :] = xin[a, 0:8, cols(g)].astype(F32)
             wk = taps(1, g)
             wv = taps(2, g)
             for lo in range(0, length, ROWS):
-                kk = causal(2 * e, wk, lo, ROWS)
-                vv = causal(2 * e + 1, wv, lo, ROWS)
-                ks[g, lo : lo + ROWS, :] = kk
-                vs[g, lo : lo + ROWS, :] = vv
-                pb[g, lo : lo + ROWS, :] = (kk * vv).astype(BF16)
-            s = mm(tailf[g, 0 : 2 * MODES], pb[g])
-            sy[0, y, p, e] = s[0:MODES] + s[MODES : 2 * MODES]
+                skipped = 8 if lo == 0 else 0
+                r = slice(lo + skipped, lo + ROWS)
+                kk = causal(2 * e, wk, lo + skipped, ROWS - skipped)
+                vv = causal(2 * e + 1, wv, lo + skipped, ROWS - skipped)
+                ks[g, r, :] = kk
+                vs[g, r, :] = vv
+                pb[g, r, :] = (kk * vv).astype(BF16)
+
+    for a in (1, 2):
+        halo_copy(a).wait_recv()
+    for g in range(groups):
+        for a in (1, 2):
+            lead[a, g, 0:8, :] = halo[a, :, cols(g)].astype(F32) * inner
+        kk = lead_rows(1, g, taps(1, g))
+        vv = lead_rows(2, g, taps(2, g))
+        ks[g, 0:8, :] = kk
+        vs[g, 0:8, :] = vv
+        pb[g, 0:8, :] = (kk * vv).astype(BF16)
+    for g in range(groups):
+        s = mm(tailf[g, 0 : 2 * MODES], pb[g])
+        sy[0, y, g // PAIR, g % PAIR] = s[0:MODES] + s[MODES : 2 * MODES]
+    for p in range(pairs):
         y_start(0, p)
 
-    @pl.loop(0, pairs)
-    def _(p):
-        y_total(0, p)
+    def before_copy(a):
+        return pltpu.make_async_remote_copy(
+            src_ref=(ks, vs)[a].at[:, pl.ds(0, 8), :],
+            dst_ref=(before_k, before_v)[a],
+            send_sem=bsend.at[a],
+            recv_sem=brecv.at[a],
+            device_id=(behind, tp),
+            device_id_type=MESH,
+        )
+
+    for a in range(2):
+        before_copy(a).start()
+
+    load(0).wait()
+    halo_copy(0).wait_recv()
+
+    @pl.loop(0, pairs)
+    def _(p):
         for e in range(PAIR):
             g = p * PAIR + e
             stage(e, 0, g)
             w = taps(0, g)
+            for lo in range(0, length, ROWS):
+                qs[g, lo : lo + ROWS, :] = causal(e, w, lo, ROWS)
+
+    tables(1)
+
+    @pl.loop(0, pairs)
+    def _(p):
+        y_total(0, p)
+        for e in range(PAIR):
+            g = p * PAIR + e
             skip = skipin[pl.ds(g, 1), :]
             for b in range(blocks):
                 r = slice(b * GROUP_CH, (b + 1) * GROUP_CH)
                 here = mm(wf[g, :, (blocks - 1 - b) * GROUP_CH :], pb[g, 0 : (b + 1) * GROUP_CH, :])
-                for lo in range(b * GROUP_CH, (b + 1) * GROUP_CH, ROWS):
-                    qs[g, lo : lo + ROWS, :] = causal(e, w, lo, ROWS)
                 fw[g, r, :] = here + skip * pb[g, r, :].astype(F32)
 
     acc[...] = jnp.zeros_like(acc)
@@ -350,12 +395,12 @@
         scales[0, r, :] = jnp.broadcast_to(scale[b : b + 1, :], (GROUP_CH, GROUP_CH)).T
         scales[1, r, :] = jnp.broadcast_to(cubed[b : b + 1, :], (GROUP_CH, GROUP_CH)).T
 
-    def edge_copy(a, g):
+    def edge_copy(p):
         return pltpu.make_async_remote_copy(
-            src_ref=(dq, dk, dv)[a].at[g, pl.ds(0, 8), :],
-            dst_ref=edge.at[a, g],
-            send_sem=gsend.at[a, g],
-            recv_sem=grecv.at[a, g],
+            src_ref=eout.at[p],
+            dst_ref=edge.at[p],
+            send_sem=gsend.at[p],
+            recv_sem=grecv.at[p],
             device_id=(behind, tp),
             device_id_type=MESH,
         )
@@ -369,37 +414,52 @@
                 r = slice(lo, lo + ROWS)
                 q = qs[g, r, :]
                 f = fw[g, r, :]
-                gated = q * f
-                scale = scales[0, r, :]
-                mixed[r, cols(g)] = (gated * scale * gain).astype(BF16)
-                d_gated = scale * (xin[3, r, cols(g)].astype(F32) * gain) - scales[1, r, :] * gated
-                dq[g, r, :] = d_gated * f
-                pb[g, r, :] = (d_gated * q).astype(BF16)
+                d_gated = scales[0, r, :] * (xin[3, r, cols(g)].astype(F32) * gain) - scales[1, r, :] * (q * f)
+                dq[g, r, :] = d_gated
+                d_filtered = (d_gated * q).astype(BF16)
+                pb[g, r, :] = d_filtered
+                if lo == 0:
+                    eout[p, 0, e] = d_gated[0:8] * f[0:8]
+                    eout[p, 1, e] = d_filtered[0:8].astype(F32)
             s = mm(tailb[g, 0 : 2 * MODES], pb[g])
             sy[1, y, p, e] = s[0:MODES] + s[MODES : 2 * MODES]
         y_start(1, p)
-        for e in range(PAIR):
-            edge_copy(0, p * PAIR + e).start()
-
-    def attach(a, g):
-        edge_copy(a, g).wait_recv()
-        (dq, dk, dv)[a][g, length : length + 8, :] = edge[a, g] * final
+        edge_copy(p).start()
+
+    @pl.loop(0, pairs)
+    def _(p):
+        for e in range(PAIR):
+            g = p * PAIR + e
+            gain = gainin[pl.ds(g, 1), :]
+            for lo in range(0, length, ROWS):
+                r = slice(lo, lo + ROWS)
+                f = fw[g, r, :]
+                mixed[r, cols(g)] = (qs[g, r, :] * f * scales[0, r, :] * gain).astype(BF16)
+                dq[g, r, :] = dq[g, r, :] * f
 
     @pl.loop(0, pairs)
     def _(p):
         y_total(1, p)
         for e in range(PAIR):
-            attach(0, p * PAIR + e)
-        for e in range(PAIR):
-            g = p * PAIR + e
-            w = taps(0, g)
+            g = p * PAIR + e
             skip = skipin[pl.ds(g, 1), :]
             for b in range(blocks):
                 r = slice(b * GROUP_CH, (b + 1) * GROUP_CH)
                 here = mm(wb[g, :, 0 : (blocks - b) * GROUP_CH], pb[g, b * GROUP_CH :, :])
-                for lo in range(b * GROUP_CH, (b + 1) * GROUP_CH, ROWS):
-                    gq[lo : lo + ROWS, cols(g)] = later(dq, g, w, lo, ROWS).astype(BF16)
                 fw[g, r, :] = here + skip * pb[g, r, :].astype(F32)
+
+    @pl.loop(0, pairs)
+    def _(p):
+        edge_copy(p).wait_recv()
+        for e in range(PAIR):
+            g = p * PAIR + e
+            dq[g, length : length + 8, :] = edge[p, 0, e] * final
+            w = taps(0, g)
+            for lo in range(0, length, ROWS):
+                gq[lo : lo + ROWS, cols(g)] = later(dq, g, w, lo, ROWS).astype(BF16)
+
+    for a in range(2):
+        before_copy(a).wait_recv()
 
     @pl.loop(0, pairs)
     def _(p):
@@ -407,19 +467,22 @@
         states_in = [entering(1, p, e) for e in range(PAIR)]
         for e in range(PAIR):
             g = p * PAIR + e
+            past = edge[p, 1, e]
+            dp = (
+                mm(ab[g, 0:8, :], states_in[e][0])
+                - mm(hneg[g], past.astype(BF16))
+                + skipin[pl.ds(g, 1), :] * past
+            ) * final
+            dk[g, length : length + 8, :] = dp * before_v[g]
+            dv[g, length : length + 8, :] = dp * before_k[g]
             for b in range(blocks):
                 r = slice(b * GROUP_CH, (b + 1) * GROUP_CH)
-                dp = fw[g, r, :] + mm(ab[g], states_in[e][b])
+                dp = fw[g, r, :] + mm(ab[g], states_in[e][b + 1])
                 dk[g, r, :] = dp * vs[g, r, :]
                 dv[g, r, :] = dp * ks[g, r, :]
-        for e in range(PAIR):
-            edge_copy(1, p * PAIR + e).start()
-            edge_copy(2, p * PAIR + e).start()
-
-    @pl.loop(0, pairs)
-    def _(p):
-        for e in range(PAIR):
-            attach(1, p * PAIR + e)
+
+    @pl.loop(0, pairs)
+    def _(p):
         for e in range(PAIR):
             g = p * PAIR + e
             w = taps(1, g)
@@ -428,6 +491,8 @@
 
     for a in range(3):
         halo_copy(a).wait_send()
+    for a in range(2):
+        before_copy(a).wait_send()
     for step in range(1, ntp):
         sums_copy(step).wait_send()
 
@@ -438,23 +503,17 @@
                 state_copy(sy, ysend, yrecv, y, d, p, step, ypeer(step)).wait_send()
             for step in range(1, NZ):
                 state_copy(sz, zsend, zrecv, z, d, p, step, zpeer(step)).wait_send()
-        for e in range(PAIR):
-            for a in range(3):
-                edge_copy(a, p * PAIR + e).wait_send()
-            attach(2, p * PAIR + e)
-
-
-def tail_kernel(mixed, gq, gk, dv, w_hbm, mixed_hbm, gq_hbm, gk_hbm, gv_hbm, win, out, sem, out_sem):
+        edge_copy(p).wait_send()
+
+
+def tail_kernel(mixed, gq, gk, dv, win, mixed_hbm, gq_hbm, gk_hbm, gv_hbm, out, sem, out_sem):
     groups, length = dv.shape[0], out.shape[1]
-    taps_in = pltpu.make_async_copy(w_hbm.at[2], win, sem.at[0])
-    taps_in.start()
     whole = [
-        pltpu.make_async_copy(src, dst, sem.at[1 + i])
+        pltpu.make_async_copy(src, dst, sem.at[i])
         for i, (src, dst) in enumerate(((mixed, mixed_hbm), (gq, gq_hbm), (gk, gk_hbm)))
     ]
     for copy in whole:
         copy.start()
-    taps_in.wait()
 
     def store(g):
         return pltpu.make_async_copy(out.at[g], gv_hbm.at[:, cols(g)], out_sem.at[g])
@@ -494,6 +553,7 @@
         vmem((groups, GROUP_CH), F32),
         vmem((3, 8, channels), BF16),
         vmem((4, length + 8, GROUP_CH), F32),
+        vmem((3, groups, 16, GROUP_CH), F32),
         vmem((groups, length, GROUP_CH), F32),
         vmem((groups, length, GROUP_CH), F32),
         vmem((groups, length, GROUP_CH), F32),
@@ -501,13 +561,17 @@
         vmem((groups, length, GROUP_CH), F32),
         vmem((groups, length + 8, GROUP_CH), F32),
         vmem((groups, length + 8, GROUP_CH), F32),
-        vmem((3, groups, 8, GROUP_CH), F32),
+        vmem((pairs, 2, PAIR, 8, GROUP_CH), F32),
+        vmem((pairs, 2, PAIR, 8, GROUP_CH), F32),
+        vmem((groups, 8, GROUP_CH), F32),
+        vmem((groups, 8, GROUP_CH), F32),
         vmem((groups, GROUP_CH, length), BF16),
         vmem((groups, GROUP_CH, length), BF16),
         vmem((groups, GROUP_CH, 3 * MODES), BF16),
         vmem((groups, GROUP_CH, 3 * MODES), BF16),
         vmem((groups, 3 * MODES, length), BF16),
         vmem((groups, 3 * MODES, length), BF16),
+        vmem((groups, 8, 8), BF16),
         vmem((states, GROUP_CH), F32),
         vmem((groups, 3 * MODES), F32),
         vmem((groups, 3 * MODES), F32),
@@ -520,7 +584,7 @@
         vmem((2, NZ, pairs, PAIR, MODES, GROUP_CH), F32),
         vmem((ntp, 8, GROUP_CH), F32),
         dma((4,)),
-        dma((5,)),
+        dma((6,)),
         dma((3,)),
         dma((3,)),
         dma((2, NY, pairs)),
@@ -529,19 +593,22 @@
         dma((2, NZ, pairs)),
         dma((ntp,)),
         dma((ntp,)),
-        dma((3, groups)),
-        dma((3, groups)),
+        dma((pairs,)),
+        dma((pairs,)),
+        dma((2,)),
+        dma((2,)),
     ]
-    mixed, gq, gk, dv = pl.pallas_call(
+    mixed, gq, gk, dv, taps = pl.pallas_call(
         functools.partial(main_kernel, ntp),
         out_shape=(
             vmem((length, channels), BF16),
             vmem((length, channels), BF16),
             vmem((length, channels), BF16),
             vmem((groups, length + 8, GROUP_CH), F32),
+            vmem(short_weight.shape[1:], F32),
         ),
         in_specs=[anywhere] * 9,
-        out_specs=(here,) * 4,
+        out_specs=(here,) * 5,
         scratch_shapes=scratch,
         compiler_params=pltpu.CompilerParams(
             collective_id=0, has_side_effects=True, vmem_limit_bytes=GRANT
@@ -555,17 +622,16 @@
     return pl.pallas_call(
         tail_kernel,
         out_shape=(result,) * 4,
-        in_specs=[here] * 4 + [anywhere],
+        in_specs=[here] * 5,
         out_specs=(anywhere,) * 4,
         scratch_shapes=[
-            vmem(short_weight.shape[1:], F32),
             vmem((groups, length, GROUP_CH), BF16),
-            dma((4,)),
+            dma((3,)),
             dma((groups,)),
         ],
         compiler_params=pltpu.CompilerParams(vmem_limit_bytes=8 * 1024 * 1024),
         name="hyena_tail",
-    )(mixed, gq, gk, dv, short_weight)
+    )(mixed, gq, gk, dv, taps)
 
 
 def solution(mesh):

time: 46.8 us -> 40.5 us (0.87)
  Pallas kernels: 45.1 us -> 39.3 us
  local copies, waits for them, and re-layouts: 0.89 us -> 0 us
    pallas_call x1, Pallas kernels: 43 us -> 37.3 us  [body(): pl.pallas_call(functools.partial(main_kernel, ntp), out_shape=(vmem((leng...]
    unnamed x2 -> x0, local copies, waits for them, and re-layouts: 0.89 us -> none
where the time goes in v3:
time: 40.5 us; the launch traced here: 40 us
  Pallas kernels  39.3 us (97%)
  between operations  0.64 us (2%)
    pallas_call x1, Pallas kernels, body(): pl.pallas_call(functools.partial(main_kernel, ntp), out_shape=(vmem((leng...  37.3 us
    pallas_call x1, Pallas kernels, body(): pl.pallas_call(tail_kernel, out_shape=(result,) * 4, in_specs=[here] * 5,...  2.09 us

profile of v3, /device:TPU:0, one launch (start us, length us, event | category | flops | bytes accessed | tf_op | source)
XLA Modules:
  0.0 40.0 jit_solution(8488695257097177997)
XLA Ops:
  0.6 37.3 %hyena_main.1 = (bf16[512,1024]{1,0:T(8,128)(2,1)S(1)}, bf16[512,1024]{1,0:T(8,128)(2,1)S(1)}, bf16[512,1024]{1,0:T(8,128)(2,1)S(1)}, f32[8,520,128]{2,1,0:T(8,128)S(1)}, f32[7,1024]{1,0:T(8,128)S(1)}) custom-call(bf16[512,1024]{1,0:T(8,128)(2,1)} %q_hbm.1, bf16[512,1024]{1,0:T(8,128)(2,1)} %k_hbm.1, bf16[512,1024]{1,0:T(8,128)(2,1)} %v_hbm.1, ...), custom_call_target="tpu_custom_call" | custom-call | tf_op jit(solution)/shard_map/hyena_main/pallas_call | solution.py:601
  37.9 2.1 %hyena_tail.1 = (bf16[512,1024]{1,0:T(8,128)(2,1)}, bf16[512,1024]{1,0:T(8,128)(2,1)}, bf16[512,1024]{1,0:T(8,128)(2,1)}, bf16[512,1024]{1,0:T(8,128)(2,1)}) custom-call(bf16[512,1024]{1,0:T(8,128)(2,1)S(1)} %get-tuple-element.9.mixed, bf16[512,1024]{1,0:T(8,128)(2,1)S(1)} %get-tuple-element.10.gq, bf16[512,1024]{1,0:T(8,128)(2,1)S(1)} %get-tuple-element.11.gk, ...), custom_call_target="tpu_custom_call" | custom-call | tf_op jit(solution)/shard_map/hyena_tail/pallas_call | solution.py:622
